TPU v7x, 128 devices: a whole 4x4x4 slice. The times are simulated.
128 devices in a mesh: dp: 8 (over z_hi, x), rows: 16 (over y, z_lo, core).
Axes of the slice: x: 4, y: 4, z: 4 (z_hi: 2, z_lo: 2; z = z_hi * 2 + z_lo), core: 2. Of those that a mesh axis runs over, the one named last changes fastest.
Arguments:
- inputs: bfloat16 [8, 512, 64, 384], P('dp', 'rows'), may hold values from -6 to 6
- cotangent: bfloat16 [8, 512, 64, 384], P('dp', 'rows'), may hold values from -6 to 6
- weight_one: bfloat16 [3456, 384], replicated, may hold values from -0.109375 to 0.109375
- weight_two: bfloat16 [3456, 384], replicated, may hold values from -0.109375 to 0.109375
Outputs:
- output: bfloat16 [8, 512, 64, 384], P('dp', 'rows')
- grad_one: float32 [3456, 384], P('rows', 'dp')
- grad_two: float32 [3456, 384], P('rows', 'dp')
All inputs are finite; a program needn't handle non-finite values.
Results may differ from a plain program's by a relative error of at most 0.006.
Values may be sent and summed in bfloat16 or wider, within the bound.
No kernel may reach another device: no remote copies, remote signals or barrier semaphores. Data moves between devices by JAX's collectives and lax.ppermute only.
A program may use at most 128 MiB of HBM per device.

v0:
```python
import math

import jax
import jax.numpy as jnp
from jax import lax
from jax.sharding import PartitionSpec as P


def padded_2(block, sides, width):
    for axis, dim in sides:
        count = lax.axis_size(axis)
        forward = [(i, i + 1) for i in range(count - 1)]
        backward = [(target, source) for source, target in forward]
        low = lax.ppermute(
            lax.slice_in_dim(block, block.shape[dim] - width, None, axis=dim), axis, forward
        )
        high = lax.ppermute(lax.slice_in_dim(block, 0, width, axis=dim), axis, backward)
        block = jnp.concatenate([low, block, high], axis=dim)
    return block


def tap_window(padded, frame, tap_number):
    count_rows, count_cols, pad_rows, pad_cols, step_rows, step_cols, direction = frame
    offset_row = tap_number // 3 - 1
    offset_col = tap_number % 3 - 1
    first_row = pad_rows + direction * offset_row * step_rows
    first_col = pad_cols + direction * offset_col * step_cols
    window = padded[first_row : first_row + count_rows, first_col : first_col + count_cols, :]
    return window.reshape(-1, padded.shape[-1])


def conv_taps(padded, frame, weights, transposed):
    channel_count = padded.shape[-1]
    summed = None
    for tap_number in range(9):
        window = tap_window(padded, frame, tap_number)
        kernel_block = weights[tap_number * channel_count : (tap_number + 1) * channel_count]
        if transposed:
            product = lax.dot_general(
                window, kernel_block, (((1,), (1,)), ((), ())), preferred_element_type=jnp.float32
            )
        else:
            product = jnp.dot(window, kernel_block, preferred_element_type=jnp.float32)
        summed = product if summed is None else summed + product
    return summed


def grad_taps(padded, frame, target):
    blocks = []
    for tap_number in range(9):
        window = tap_window(padded, frame, tap_number)
        blocks.append(
            lax.dot_general(
                window, target, (((0,), (0,)), ((), ())), preferred_element_type=jnp.float32
            )
        )
    return jnp.concatenate(blocks, axis=0)


def reduce_grad(partial_grad):
    shared = lax.psum_scatter(partial_grad, "rows", scatter_dimension=0, tiled=True)
    return lax.psum_scatter(shared, "dp", scatter_dimension=1, tiled=True)


def on_device(inputs, cotangent, weight_one, weight_two):
    picture = inputs[0]
    upstream_gradient = cotangent[0]
    row_count, col_count, channel_count = picture.shape
    group_size = lax.axis_size("rows")
    spacing = 2 * group_size
    factor = 1.0 / math.sqrt(lax.axis_size("dp") * row_count * group_size * col_count)
    rimmed = padded_2(picture, (("rows", 0),), 4)
    rimmed = jnp.pad(rimmed, ((0, 0), (4, 4), (0, 0)))
    near_frame = (row_count, col_count, 4, 4, 4, 4, 1)
    before = conv_taps(rimmed, near_frame, weight_one, False)
    hidden_state = (
        jnp.maximum(before, 0.0).astype(jnp.bfloat16).reshape(row_count, col_count, channel_count)
    )
    moved = (
        lax.all_to_all(
            hidden_state.reshape(row_count // group_size, group_size, col_count, channel_count),
            "rows",
            split_axis=1,
            concat_axis=0,
            tiled=True,
        ),
        lax.all_to_all(
            upstream_gradient.reshape(
                row_count // group_size, group_size, col_count, channel_count
            ),
            "rows",
            split_axis=1,
            concat_axis=0,
            tiled=True,
        ),
    )
    hidden_cyc = moved[0].reshape(row_count, col_count, channel_count)
    upstream_cyc = moved[1].reshape(row_count, col_count, channel_count)
    widths = ((2, 2), (spacing, spacing), (0, 0))
    hidden_pad = jnp.pad(hidden_cyc, widths)
    far_frame = (row_count, col_count, 2, spacing, 2, spacing, 1)
    result = conv_taps(hidden_pad, far_frame, weight_two, False).astype(jnp.bfloat16)
    output = lax.all_to_all(
        result.reshape(group_size, row_count // group_size, 1, col_count, channel_count),
        "rows",
        split_axis=0,
        concat_axis=2,
        tiled=True,
    ).reshape(row_count, col_count, channel_count)
    grad_two = reduce_grad(
        grad_taps(hidden_pad, far_frame, upstream_cyc.reshape(-1, channel_count))
    )
    mirror_frame = (row_count, col_count, 2, spacing, 2, spacing, -1)
    back_cyc = conv_taps(jnp.pad(upstream_cyc, widths), mirror_frame, weight_two, True).astype(
        jnp.bfloat16
    )
    backward_signal = lax.all_to_all(
        back_cyc.reshape(group_size, row_count // group_size, 1, col_count, channel_count),
        "rows",
        split_axis=0,
        concat_axis=2,
        tiled=True,
    ).reshape(-1, channel_count)
    masked = jnp.where(before > 0.0, backward_signal, jnp.zeros_like(backward_signal))
    grad_one = reduce_grad(grad_taps(rimmed, near_frame, masked))
    return (output[None], grad_one * factor, grad_two * factor)


def solution(mesh):
    return jax.shard_map(
        on_device,
        mesh=mesh,
        in_specs=(P("dp", "rows", None, None), P("dp", "rows", None, None), P(), P()),
        out_specs=(P("dp", "rows", None, None), P("rows", "dp"), P("rows", "dp")),
        check_vma=False,
    )
```

profile of v0, /device:TPU:0, one launch (start us, length us, event | category | flops | bytes accessed | tf_op | source)
XLA Modules:
  0.0 480.7 jit_solution(16997275604997559880)
XLA Ops:
  9.9 6.2 %all-to-all-start.2 = ((bf16[2,16,64,384]{3,2,0,1:T(8,128)(2,1)}), bf16[2,16,64,384]{3,2,0,1:T(8,128)(2,1)S(1)}, u32[]{:S(2)}, u32[]{:S(2)}) async-start(bf16[2,16,64,384]{3,2,0,1:T(8,128)(2,1)} %copy.28), calls=%async_computation.2 | async-start | bytes 3145728 | tf_op jit(solution)/shard_map/all_to_all | solution.py:87
  19.8 3.7 fusion.27
  28.5 3.9 fusion.20
  32.5 3.8 fusion.23
  36.3 3.8 fusion.25
  40.1 3.6 pad_slice_fusion
  56.3 3.8 fusion.63
  60.1 3.7 fusion.67
  63.8 7.0 %add_convert_fusion = bf16[2048,384]{1,0:T(8,128)(2,1)} fusion(f32[2048,384]{1,0:T(8,128)S(1)} %fusion.39, f32[2048,384]{1,0:T(8,128)S(1)} %fusion.43, f32[2048,384]{1,0:T(8,128)S(1)} %fusion.47, f32[2048,384]{1,0:T(8,128)S(1)} %fusion.51, f32[2048,384]{1,0:T(8,128)S(1)} %fusion.55, f32[2048,384]{1,0:T(8,128)S(1)} %fusion.59, f32[2048,384]{1,0:T(8,128)} %fusion.67, ...), kind=kOutput, calls=%fused_computation.19 | convolution fusion | flops 611057664 | bytes 28606464 | tf_op jit(solution)/shard_map/dot_general | solution.py:39
  70.9 20.8 %all-to-all-start.3 = ((bf16[16,2,1,64,384]{4,3,1,2,0:T(8,128)(2,1)}), bf16[16,2,1,64,384]{4,3,1,2,0:T(8,128)(2,1)}, u32[]{:S(2)}, u32[]{:S(2)}) async-start(bf16[16,2,1,64,384]{4,3,1,2,0:T(8,128)(2,1)} %bitcast.211), calls=%async_computation.3 | async-start | bytes 3145728 | tf_op jit(solution)/shard_map/all_to_all | solution.py:117
  93.8 4.0 fusion.29
  97.9 3.8 fusion.31
  101.7 3.8 fusion.35
  105.5 3.8 fusion.33
  109.3 4.6 all-to-all-done.3
  116.2 11.4 %compare_select_fusion = (bf16[2048,384]{1,0:T(8,128)(2,1)S(1)}, bf16[2048,384]{1,0:T(8,128)(2,1)}) fusion(bf16[1,2,16,1,64,384]{5,4,2,1,3,0:T(8,128)(2,1)S(1)} %copy.30, f32[2048,384]{1,0:T(8,128)} %fusion.20, bf16[2048,384]{1,0:T(8,128)(2,1)} %bitcast.198, bf16[3456,384]{1,0:T(8,128)(2,1)} %param.6, f32[2048,384]{1,0:T(8,128)} %fusion.23, ...), kind=kOutput, calls=%fused_computation.23 | convolution fusion | flops 613416960 | bytes 31752192 | tf_op jit(solution)/shard_map/dot_general | solution.py:43
  145.9 29.6 %all_to_all.60 = bf16[2,16,64,384]{3,2,0,1:T(8,128)(2,1)S(1)} all-to-all(bf16[2,16,64,384]{3,2,0,1:T(8,128)(2,1)S(1)} %copy.25), channel_id=1, replica_groups=mesh['dp'=8,'rows'=16] {'rows'}, dimensions={1} | all-to-all | bytes 3145728 | tf_op jit(solution)/shard_map/all_to_all | solution.py:80
  175.5 3.1 pad_slice_fusion.8
  213.0 6.6 %add_convert_fusion.1 = bf16[2048,384]{1,0:T(8,128)(2,1)} fusion(f32[2048,384]{1,0:T(8,128)S(1)} %fusion.41, f32[2048,384]{1,0:T(8,128)S(1)} %fusion.45, f32[2048,384]{1,0:T(8,128)S(1)} %fusion.49, f32[2048,384]{1,0:T(8,128)} %fusion.53, f32[2048,384]{1,0:T(8,128)S(1)} %fusion.57, f32[2048,384]{1,0:T(8,128)S(1)} %fusion.61, f32[2048,384]{1,0:T(8,128)} %fusion.69, ...), kind=kOutput, calls=%fused_computation.20 | convolution fusion | flops 611057664 | bytes 28606464 | tf_op jit(solution)/shard_map/dot_general | solution.py:43
  219.6 4.7 all-to-all-start.1
  224.4 4.9 %reduce-scatter.19.cloned.1.call-done = f32[216,384]{1,0:T(8,128)} async-done(((f32[3456,384]{1,0:T(8,128)}), f32[216,384]{1,0:T(8,128)}) %reduce-scatter.19.cloned.1.call-update) | async-done | bytes 331792
  231.2 88.9 %reduce-scatter.21.cloned.1.call-done = f32[216,384]{1,0:T(8,128)} async-done(((f32[3456,384]{1,0:T(8,128)}), f32[216,384]{1,0:T(8,128)}) %reduce-scatter.21.cloned.1.call-update) | async-done | bytes 331792
  323.3 74.7 %reduce-scatter.15.cloned.1.call-done = f32[48,216]{1,0:T(8,128)} async-done(((f32[384,216]{1,0:T(8,128)}), f32[48,216]{1,0:T(8,128)}) %reduce-scatter.15.cloned.1.call-update) | async-done | bytes 41488
  399.6 72.8 %reduce-scatter.17.cloned.1.call-done = f32[48,216]{1,0:T(8,128)} async-done(((f32[384,216]{1,0:T(8,128)}), f32[48,216]{1,0:T(8,128)}) %reduce-scatter.17.cloned.1.call-update) | async-done | bytes 41488
  (132 shorter events, 89.5 us)
Async XLA Ops:
  9.9 6.2 %copy-start = (bf16[1,32,64,384]{3,2,1,0:T(8,128)(2,1)S(1)}, bf16[1,32,64,384]{3,2,1,0:T(8,128)(2,1)}, u32[]{:S(2)}) copy-start(bf16[1,32,64,384]{3,2,1,0:T(8,128)(2,1)} %param.4) | copy-start | bytes 4718596
  9.9 30.2 %all-to-all-start.2 = ((bf16[2,16,64,384]{3,2,0,1:T(8,128)(2,1)}), bf16[2,16,64,384]{3,2,0,1:T(8,128)(2,1)S(1)}, u32[]{:S(2)}, u32[]{:S(2)}) async-start(bf16[2,16,64,384]{3,2,0,1:T(8,128)(2,1)} %copy.28), calls=%async_computation.2 | async-start | bytes 3145728 | tf_op jit(solution)/shard_map/all_to_all | solution.py:87
  16.2 7.3 %collective-permute-start = (bf16[4,64,384]{2,1,0:T(8,128)(2,1)S(1)}, bf16[4,64,384]{2,1,0:T(8,128)(2,1)S(1)}, u32[]{:S(2)}, u32[]{:S(2)}) collective-permute-start(bf16[4,64,384]{2,1,0:T(8,128)(2,1)S(1)} %get-tuple-element.41), channel_id=1, source_target_pairs={{0,1},{1,2},{2,3},{3,4},{4,5},{5,6},{6,7},{7,8},{8,9},{9,10},{10,1... | collective-permute-start | bytes 589832 | tf_op jit(solution)/shard_map/ppermute | solution.py:14
  18.5 5.0 %collective-permute-start.1 = (bf16[4,64,384]{2,1,0:T(8,128)(2,1)S(1)}, bf16[4,64,384]{2,1,0:T(8,128)(2,1)S(1)}, u32[]{:S(2)}, u32[]{:S(2)}) collective-permute-start(bf16[4,64,384]{2,1,0:T(8,128)(2,1)S(1)} %get-tuple-element.42), channel_id=1, source_target_pairs={{1,0},{2,1},{3,2},{4,3},{5,4},{6,5},{7,6},{8,7},{9,8},{10,9},{11,1... | collective-permute-start | bytes 589832 | tf_op jit(solution)/shard_map/ppermute | solution.py:17
  28.5 4.0 copy-start.2
  28.5 4.0 copy-start.4
  28.5 7.8 %copy-start.6 = (bf16[32,64,384]{2,1,0:T(8,128)(2,1)}, bf16[32,64,384]{2,1,0:T(8,128)(2,1)S(1)}, u32[]{:S(2)}) copy-start(bf16[32,64,384]{2,1,0:T(8,128)(2,1)S(1)} %get-tuple-element.19) | copy-start | bytes 4718596
  70.9 43.0 %all-to-all-start.3 = ((bf16[16,2,1,64,384]{4,3,1,2,0:T(8,128)(2,1)}), bf16[16,2,1,64,384]{4,3,1,2,0:T(8,128)(2,1)}, u32[]{:S(2)}, u32[]{:S(2)}) async-start(bf16[16,2,1,64,384]{4,3,1,2,0:T(8,128)(2,1)} %bitcast.211), calls=%async_computation.3 | async-start | bytes 3145728 | tf_op jit(solution)/shard_map/all_to_all | solution.py:117
  91.7 137.5 %reduce-scatter.19.cloned.1.call-start = ((), (), s32[]{:S(2)}) async-start(), calls=%async_computation.10 | async-start | bytes 5640192
  93.7 11.8 %copy-start.28 = (bf16[32,64,384]{2,1,0:T(8,128)(2,1)}, bf16[32,64,384]{2,1,0:T(8,128)(2,1)S(1)}, u32[]{:S(2)}) copy-start(bf16[32,64,384]{2,1,0:T(8,128)(2,1)S(1)} %get-tuple-element.40) | copy-start | bytes 4718596
  93.8 4.0 copy-start.10
  97.9 3.9 copy-start.12
  116.2 11.4 %copy-start.13 = (bf16[32,64,384]{2,1,0:T(8,128)(2,1)S(1)}, bf16[32,64,384]{2,1,0:T(8,128)(2,1)}, u32[]{:S(2)}) copy-start(bf16[32,64,384]{2,1,0:T(8,128)(2,1)} %get-tuple-element.17) | copy-start | bytes 4718596
  144.3 175.7 %reduce-scatter.21.cloned.1.call-start = ((), (), s32[]{:S(2)}) async-start(), calls=%async_computation.11 | async-start | bytes 5640192
  178.6 4.9 %copy-start.18 = (bf16[32,64,384]{2,1,0:T(8,128)(2,1)}, bf16[32,64,384]{2,1,0:T(8,128)(2,1)S(1)}, u32[]{:S(2)}) copy-start(bf16[32,64,384]{2,1,0:T(8,128)(2,1)S(1)} %get-tuple-element.33) | copy-start | bytes 4718596
  178.6 6.7 %copy-start.20 = (bf16[32,64,384]{2,1,0:T(8,128)(2,1)}, bf16[32,64,384]{2,1,0:T(8,128)(2,1)S(1)}, u32[]{:S(2)}) copy-start(bf16[32,64,384]{2,1,0:T(8,128)(2,1)S(1)} %get-tuple-element.34) | copy-start | bytes 4718596
  178.6 10.5 %copy-start.22 = (bf16[32,64,384]{2,1,0:T(8,128)(2,1)}, bf16[32,64,384]{2,1,0:T(8,128)(2,1)S(1)}, u32[]{:S(2)}) copy-start(bf16[32,64,384]{2,1,0:T(8,128)(2,1)S(1)} %get-tuple-element.35) | copy-start | bytes 4718596
  178.6 12.4 %copy-start.24 = (bf16[32,64,384]{2,1,0:T(8,128)(2,1)}, bf16[32,64,384]{2,1,0:T(8,128)(2,1)S(1)}, u32[]{:S(2)}) copy-start(bf16[32,64,384]{2,1,0:T(8,128)(2,1)S(1)} %get-tuple-element.36) | copy-start | bytes 4718596
  178.6 14.2 %copy-start.26 = (bf16[32,64,384]{2,1,0:T(8,128)(2,1)}, bf16[32,64,384]{2,1,0:T(8,128)(2,1)S(1)}, u32[]{:S(2)}) copy-start(bf16[32,64,384]{2,1,0:T(8,128)(2,1)S(1)} %get-tuple-element.37) | copy-start | bytes 4718596
  178.7 16.1 %copy-start.31 = (bf16[32,64,384]{2,1,0:T(8,128)(2,1)}, bf16[32,64,384]{2,1,0:T(8,128)(2,1)S(1)}, u32[]{:S(2)}) copy-start(bf16[32,64,384]{2,1,0:T(8,128)(2,1)S(1)} %get-tuple-element.31) | copy-start | bytes 4718596
  210.2 2.8 copy-start.32
  219.6 102.4 %all-to-all-start.1 = ((bf16[16,2,1,64,384]{4,3,1,2,0:T(8,128)(2,1)}), bf16[16,2,1,64,384]{4,3,1,2,0:T(8,128)(2,1)S(1)}, u32[]{:S(2)}, u32[]{:S(2)}) async-start(bf16[16,2,1,64,384]{4,3,1,2,0:T(8,128)(2,1)} %bitcast.27), calls=%async_computation.1 | async-start | bytes 3145728 | tf_op jit(solution)/shard_map/all_to_all | solution.py:103
  224.3 173.7 %reduce-scatter.15.cloned.1.call-start = ((), (), s32[]{:S(2)}) async-start(), calls=%async_computation.8 | async-start | bytes 442368
  231.1 241.3 %reduce-scatter.17.cloned.1.call-start = ((), (), s32[]{:S(2)}) async-start(), calls=%async_computation.9 | async-start | bytes 442368
  (20 other events, 36.4 us)
Sparse Core Ops, SparseCore 0:
  144.5 84.7 reduce-scatter.18
  231.6 88.3 reduce-scatter.20
  323.7 74.2 reduce-scatter.14
  401.4 70.8 reduce-scatter.16
where the time goes:
time: 488 us; the launch traced here: 481 us
  waiting for transfers between devices  246 us (50%)
  matrix products  124 us (25%)
  starting transfers between devices  35.9 us (7%)
  blocking collectives  29.6 us (6%)
  local copies, waits for them, and re-layouts  27.4 us (6%)
  between operations  14.3 us (3%)
    unnamed x8, waiting for transfers between devices  241 us
    dot_general x18, matrix products, conv_taps(): product = jnp.dot(window, kernel_block, preferred_element_type=jnp.float32)  62.2 us
    dot_general x18, matrix products, grad_taps(): lax.dot_general(window, target, (((0,), (0,)), ((), ())), preferred_eleme...  34.5 us
    all_to_all x1, blocking collectives, on_device(): lax.all_to_all(hidden_state.reshape(row_count // group_size, group_size,...  29.6 us
    dot_general x9, matrix products, conv_taps(): lax.dot_general(window, kernel_block, (((1,), (1,)), ((), ())), preferred...  27.1 us
    all_to_all x1, starting transfers between devices, on_device(): lax.all_to_all(back_cyc.reshape(group_size, row_count // group_size, 1, c...  20.8 us
    unnamed x76, local copies, waits for them, and re-layouts  12 us
  transfers between devices with their start and end apart: 9, of which 5 were waited for; matrix products, arithmetic and copies ran while one was open for 18% of the time, Pallas kernels for 0%

commit v1 on v0

v1 whole, which is shorter than its diff:
```python
import functools
import math

import jax
import jax.numpy as jnp
from jax import lax
from jax.experimental import pallas as pl
from jax.experimental.pallas import tpu as pltpu
from jax.sharding import PartitionSpec as P


F32 = jnp.float32
BF16 = jnp.bfloat16
CH = 384
ROWS = 32
COLS = 64
HALF = 32
TAPS = 9 * CH
BLOCK = 216
SLIM = 48
WHOLE = pl.BlockSpec(memory_space=pltpu.VMEM)
AXES = ("dp", "rows")


def call(kernel, outs, args, flops=0, scratch=(), limit=8, aliases=None):
    single = not isinstance(outs, (list, tuple))
    shapes = [outs] if single else list(outs)
    moved = sum(a.size * a.dtype.itemsize for a in list(args) + shapes)
    run = pl.pallas_call(
        kernel,
        out_shape=shapes,
        in_specs=[WHOLE] * len(args),
        out_specs=[WHOLE] * len(shapes),
        scratch_shapes=list(scratch),
        input_output_aliases=aliases or {},
        compiler_params=pltpu.CompilerParams(vmem_limit_bytes=limit << 20),
        cost_estimate=pl.CostEstimate(flops=flops, bytes_accessed=moved, transcendentals=0),
    )
    result = run(*args)
    return result[0] if single else result


def shape_of(dims, kind):
    return jax.ShapeDtypeStruct(dims, kind)


def matmul(left, right):
    return jnp.dot(left, right, preferred_element_type=F32)


def place():
    dp = lax.axis_index("dp")
    rows = lax.axis_index("rows")
    return (
        lax.rem(dp, 4),
        lax.div(rows, 4),
        lax.rem(lax.div(rows, 2), 2),
        lax.div(dp, 4),
        lax.rem(rows, 2),
    )


def pairs_of(move):
    found = []
    for x in range(4):
        for y in range(4):
            for low in range(2):
                for high in range(2):
                    for core in range(2):
                        tx, ty, tl, th, tc = move(x, y, low, high, core)
                        source = (high * 4 + x) * 16 + (y * 2 + low) * 2 + core
                        target = (th * 4 + tx % 4) * 16 + ((ty % 4) * 2 + tl) * 2 + tc
                        found.append((source, target))
    return found


def send(block, move):
    return lax.ppermute(block, AXES, pairs_of(move))


def weight_kernel(w_ref, forward_ref, backward_ref):
    for a in range(3):
        zero = w_ref[pl.ds((3 * a + 1) * CH, CH)]
        minus = w_ref[pl.ds(3 * a * CH, CH)]
        plus = w_ref[pl.ds((3 * a + 2) * CH, CH)]
        parts = ((zero, minus), (plus, zero))
        for i in range(2):
            for j in range(2):
                forward_ref[pl.ds((2 * a + i) * CH, CH), pl.ds(j * CH, CH)] = parts[i][j]
                backward_ref[pl.ds((2 * a + j) * CH, CH), pl.ds(i * CH, CH)] = parts[i][j].T


def shifted_store(near_ref, first, value):
    count = value.shape[0]
    zeros = jnp.zeros((count, 4, CH), BF16)
    near_ref[0, pl.ds(first, count)] = jnp.concatenate([zeros, value[:, : COLS - 4]], axis=1)
    near_ref[1, pl.ds(first, count)] = value
    near_ref[2, pl.ds(first, count)] = jnp.concatenate([value[:, 4:], zeros], axis=1)


def near_rows(near_ref, w_ref, hidden_ref, first, count):
    total = None
    for a in range(3):
        for b in range(3):
            window = near_ref[b, pl.ds(first + 4 * a, count)].reshape(count * COLS, CH)
            product = matmul(window, w_ref[pl.ds((3 * a + b) * CH, CH)])
            total = product if total is None else total + product
    hidden_ref[pl.ds(first, count)] = (
        jnp.maximum(total, 0.0).astype(BF16).reshape(count, COLS, CH)
    )


def near_mid_kernel(own_ref, w_ref, hidden_ref, near_ref):
    @pl.loop(0, ROWS // 4)
    def _(i):
        shifted_store(near_ref, 4 + i * 4, own_ref[pl.ds(i * 4, 4)])

    @pl.loop(0, 3)
    def _(m):
        near_rows(near_ref, w_ref, hidden_ref, 4 + m * 8, 8)


def near_edge_kernel(distant_ref, chip_ref, w_ref, mid_ref, wide_ref, hidden_ref, near_ref):
    core = place()[4]
    shifted_store(near_ref, (ROWS + 4) * core, distant_ref[...])
    shifted_store(near_ref, (ROWS + 4) * (1 - core), chip_ref[...])

    @pl.loop(0, 2)
    def _(m):
        near_rows(near_ref, w_ref, hidden_ref, m * (ROWS - 4), 4)


def side_rows(ref, first, chunk):
    return jnp.concatenate(
        [
            ref[pl.ds(first, chunk), pl.ds(side * HALF, HALF)].reshape(chunk * HALF, CH)
            for side in range(2)
        ],
        axis=1,
    )


def block_of(w_ref, at):
    return w_ref[pl.ds(pl.multiple_of(at * 2 * CH, 16), 2 * CH)]


def far_start_kernel(flip, own_ref, chip_ref, w_ref, total_ref):
    core = place()[4]
    at = 2 * core if flip else 2 - 2 * core
    chunk = 16

    @pl.loop(0, ROWS // chunk)
    def _(m):
        total = matmul(side_rows(own_ref, m * chunk, chunk), block_of(w_ref, 1))
        total = total + matmul(side_rows(chip_ref, m * chunk, chunk), block_of(w_ref, at))
        for side in range(2):
            total_ref[pl.ds(m * chunk, chunk), pl.ds(side * HALF, HALF)] = total[
                :, side * CH : (side + 1) * CH
            ].reshape(chunk, HALF, CH)


PART = ROWS // 2


def distant_part(distant_ref, w_ref, at, first, chunk):
    return matmul(side_rows(distant_ref, first, chunk), block_of(w_ref, at))


def conv_end_kernel(total_ref, distant_ref, w_ref, out_ref):
    core = place()[4]
    chunk = 16

    @pl.loop(0, ROWS // chunk)
    def _(m):
        total = distant_part(distant_ref, w_ref, 2 * core, m * chunk, chunk)
        for side in range(2):
            where = (pl.ds(m * chunk, chunk), pl.ds(side * HALF, HALF))
            part = total[:, side * CH : (side + 1) * CH].reshape(chunk, HALF, CH)
            out_ref[where] = (total_ref[where] + part).astype(BF16)


def back_end_kernel(index, total_ref, distant_ref, w_ref, hidden_ref, out_ref):
    core = place()[4]
    total = distant_part(distant_ref, w_ref, 2 - 2 * core, 0, PART)
    for side in range(2):
        cols = slice(side * HALF, (side + 1) * HALF)
        where = (slice(index * PART, (index + 1) * PART), cols)
        part = total[:, side * CH : (side + 1) * CH].reshape(PART, HALF, CH)
        value = (total_ref[where] + part).astype(BF16)
        out_ref[:, cols] = jnp.where(hidden_ref[where] > 0, value, jnp.zeros_like(value))


def split_cores(full_ref, keep_ref, send_ref):
    core = place()[4]
    for j in range(8):
        mine = full_ref[pl.ds(pl.multiple_of((2 * j + core) * BLOCK, 8), BLOCK)]
        other = full_ref[pl.ds(pl.multiple_of((2 * j + 1 - core) * BLOCK, 8), BLOCK)]
        keep_ref[j // 2, j % 2] = mine
        send_ref[j // 2, j % 2] = other.astype(BF16)


def outer(left, right):
    return lax.dot_general(left, right, (((0,), (0,)), ((), ())), preferred_element_type=F32)


def fill_halves(ref, out_ref):
    for side in range(2):
        out_ref[:, side * CH : (side + 1) * CH] = ref[
            :, side * HALF : (side + 1) * HALF
        ].reshape(ROWS * HALF, CH)


def taps_at(full_ref, at):
    return full_ref.at[pl.ds(pl.multiple_of(at * 3 * CH, 16), 3 * CH)]


def outer_taps(h_ref, c_ref, target):
    grad = outer(h_ref[...], c_ref[...])
    target[0:CH] = grad[:CH, CH:]
    target[CH : 2 * CH] = grad[:CH, :CH] + grad[CH:, CH:]
    target[2 * CH :] = grad[CH:, :CH]


def grad_start_kernel(hidden_ref, own_ref, chip_ref, full_ref, h_ref, c_ref):
    core = place()[4]
    fill_halves(hidden_ref, h_ref)
    fill_halves(own_ref, c_ref)
    outer_taps(h_ref, c_ref, taps_at(full_ref, 1))
    fill_halves(chip_ref, c_ref)
    outer_taps(h_ref, c_ref, taps_at(full_ref, 2 * core))


def fill_part(ref, first, out_ref):
    for side in range(2):
        out_ref[:, side * CH : (side + 1) * CH] = ref[
            first : first + PART, side * HALF : (side + 1) * HALF
        ].reshape(PART * HALF, CH)


def grad_part_kernel(hidden_ref, distant_ref, part_ref, h_ref, c_ref):
    fill_part(hidden_ref, 0, h_ref)
    fill_part(distant_ref, 0, c_ref)
    outer_taps(h_ref, c_ref, part_ref)


def grad_end_kernel(
    begun_ref, part_ref, hidden_ref, distant_ref, keep_ref, send_ref, h_ref, c_ref, full_ref
):
    core = place()[4]
    fill_part(hidden_ref, PART, h_ref)
    fill_part(distant_ref, 0, c_ref)
    target = taps_at(full_ref, 2 - 2 * core)
    outer_taps(h_ref, c_ref, target)
    target[...] = target[...] + part_ref[...]
    for at in (1, 2 * core):
        taps_at(full_ref, at)[...] = taps_at(begun_ref, at)[...]
    split_cores(full_ref, keep_ref, send_ref)


def near_window(near_ref, index, a, b):
    first = 4 * a + index * PART
    return near_ref[b, first : first + PART].reshape(PART * COLS, CH)


def near_part_kernel(near_ref, masked_ref, part_ref):
    target = masked_ref[...].reshape(PART * COLS, CH)
    for a in range(3):
        for b in range(3):
            part_ref[pl.ds((3 * a + b) * CH, CH)] = outer(near_window(near_ref, 0, a, b), target)


def near_end_kernel(part_ref, near_ref, masked_ref, keep_ref, send_ref, full_ref):
    target = masked_ref[...].reshape(PART * COLS, CH)
    for a in range(3):
        for b in range(3):
            where = pl.ds((3 * a + b) * CH, CH)
            full_ref[where] = part_ref[where] + outer(near_window(near_ref, 1, a, b), target)
    split_cores(full_ref, keep_ref, send_ref)


BANDS = tuple((at, min(48, BLOCK - at)) for at in range(0, BLOCK, 48))


def one_first_kernel(keep_ref, got_ref, own_ref, p1, p2, p3, hold_ref):
    x = place()[0]
    for at, count in BANDS:
        band = slice(at, at + count)
        lane = lax.broadcasted_iota(jnp.int32, (count, CH), 1)
        lane = jnp.where(lane >= 4 * SLIM, lane - 4 * SLIM, lane)
        for low in range(2):
            turned = []
            for y in range(4):
                total = keep_ref[y, low, band] + got_ref[y, low, band].astype(F32)
                turned.append(pltpu.roll(total, SLIM * y, 1) if y else total)
            for q in range(4):
                part = turned[(3 - q) % 4]
                for r in (2, 1, 0):
                    part = jnp.where(lane < (r + 1) * SLIM, turned[(r - q) % 4], part)
                hold_ref[q, low, band] = part
    own_ref[...] = hold_ref[x]
    for k, ref in enumerate((p1, p2, p3)):
        ref[...] = hold_ref[lax.rem(x + k + 1, 4)].astype(BF16)


def two_first_kernel(keep_ref, got_ref, *refs):
    y = place()[1]
    for k, ref in enumerate(refs):
        at = lax.rem(y + k, 4)
        ref[...] = (keep_ref[at] + got_ref[at].astype(F32)).astype(ref.dtype)


def second_kernel(turned, kept_ref, r1, r2, r3, own_ref, p1, p2, p3, hold_ref):
    x, y = place()[:2]
    base = x + y if turned else x
    for at, count in BANDS:
        band = slice(at, at + count)
        for low in range(2):
            total = kept_ref[low, band]
            for r in (r1, r2, r3):
                total = total + r[low, band].astype(F32)
            for q in range(4):
                for side in range(2):
                    start = side * 4 * SLIM + q * SLIM
                    to = (2 * low + side) * SLIM
                    hold_ref[q, band, to : to + SLIM] = total[:, start : start + SLIM]
    own_ref[...] = hold_ref[lax.rem(base, 4)]
    for k, ref in enumerate((p1, p2, p3)):
        ref[...] = hold_ref[lax.rem(base + k + 1, 4)].astype(BF16)


def third_kernel(*refs):
    ins, (own_ref, p1, p2, p3, hold_ref) = refs[:8], refs[8:]
    x, y, low, high, _ = place()
    for g in range(2):
        kept, *got = ins[4 * g : 4 * g + 4]
        total = kept[...]
        for ref in got:
            total = total + ref[...].astype(F32)
        for l in range(2):
            for side in range(2):
                at = (2 * l + side) * SLIM
                hold_ref[g, l, side] = total[:, at : at + SLIM]
        here = high if g else lax.rem(high + lax.div(x + y, 4), 2)
        spots = ((low, here), (1 - low, here), (low, 1 - here), (1 - low, 1 - here))
        for ref, (l, side) in zip((own_ref, p1, p2, p3), spots):
            ref[:, g * SLIM : (g + 1) * SLIM] = hold_ref[g, l, side].astype(ref.dtype)


def last_kernel(factor, kept_ref, r1, r2, r3, one_ref, two_ref):
    total = kept_ref[...]
    for ref in (r1, r2, r3):
        total = total + ref[...].astype(F32)
    total = total * factor
    one_ref[...] = total[:, 0:SLIM]
    two_ref[...] = total[:, SLIM : 2 * SLIM]


def pieces_of(dims):
    return [shape_of(dims, F32)] + [shape_of(dims, BF16)] * 3


def swap_core(block):
    return send(block, lambda x, y, l, h, c: (x, y, l, h, 1 - c))


def over_x(pieces):
    own, *pieces = pieces
    result = [own]
    for k, piece in enumerate(pieces):
        result.append(send(piece, lambda x, y, l, h, c: (x + k + 1, y, l, h, c)))
    return result


def over_y(pieces):
    own, *pieces = pieces
    result = [own]
    for k, piece in enumerate(pieces):
        result.append(send(piece, lambda x, y, l, h, c: (x, y + k + 1, l, h, c)))
    return result


def second_stage(turned, held):
    dims = (BLOCK, 4 * SLIM)
    return call(
        functools.partial(second_kernel, turned),
        pieces_of(dims),
        held,
        scratch=[pltpu.VMEM((4, *dims), F32)],
    )


def reduce_grads(keep_one, send_one, keep_two, send_two, factor):
    got_one = swap_core(send_one)
    got_two = swap_core(send_two)
    dims = (2, BLOCK, CH)
    one = call(
        one_first_kernel,
        pieces_of(dims),
        (keep_one, got_one),
        scratch=[pltpu.VMEM((4, *dims), F32)],
    )
    two = call(two_first_kernel, pieces_of(dims), (keep_two, got_two))
    one = second_stage(True, over_x(one))
    two = second_stage(False, over_y(two))
    one = over_y(one)
    two = over_x(two)
    dims = (BLOCK, 2 * SLIM)
    own, *pieces = call(
        third_kernel,
        pieces_of(dims),
        (*one, *two),
        scratch=[pltpu.VMEM((2, 2, 2, BLOCK, SLIM), F32)],
    )
    moves = (
        lambda x, y, l, h, c: (x, y, 1 - l, h, c),
        lambda x, y, l, h, c: (x, y, l, 1 - h, c),
        lambda x, y, l, h, c: (x, y, 1 - l, 1 - h, c),
    )
    got = []
    for piece, move in zip(pieces, moves):
        got.append(send(piece, move))
    kind = shape_of((BLOCK, SLIM), F32)
    return call(functools.partial(last_kernel, factor), [kind, kind], (own, *got))


def swap_chip(block):
    return send(block, lambda x, y, l, h, c: (x, y, l, h, 1 - c))


def swap_distant(block):
    count = lax.axis_size("rows")
    pairs = [(i, i + 1) for i in range(1, count - 1, 2)]
    return lax.ppermute(block, "rows", pairs + [(j, i) for i, j in pairs])


def swap_in_steps(block):
    count = lax.axis_size("rows")
    pairs = [(i, i) for i in range(count) if i % 4 in (1, 2)]
    for i in range(3, count - 1, 4):
        pairs += [(i, i + 4), (i + 1, i - 3)]
    block = lax.ppermute(block, "rows", pairs)
    return lax.ppermute(block, "rows", [(i, i ^ 3) for i in range(count)])


def on_device(inputs, cotangent, weight_one, weight_two):
    picture = inputs[0]
    upstream = cotangent[0]
    factor = 1.0 / math.sqrt(lax.axis_size("dp") * ROWS * lax.axis_size("rows") * COLS)
    work = 2 * ROWS * COLS * CH * CH
    first_core = lax.rem(lax.axis_index("rows"), 2) == 0
    head, tail = picture[:4], picture[-4:]
    edge_distant = swap_distant(jnp.where(first_core, head, tail))
    c_parts = [swap_distant(upstream[i * PART : (i + 1) * PART]) for i in range(2)]
    edge_chip = swap_chip(jnp.where(first_core, tail, head))
    c_chip = swap_chip(upstream)
    kind = shape_of((6 * CH, 2 * CH), BF16)
    forward_w, backward_w = call(weight_kernel, [kind, kind], (weight_two,))
    map_kind = shape_of((ROWS, COLS, CH), BF16)
    part_kind = shape_of((PART, COLS, CH), BF16)
    sum_kind = shape_of((ROWS, COLS, CH), F32)
    wide_kind = shape_of((3, ROWS + 8, COLS, CH), BF16)
    hidden, near = call(
        near_mid_kernel, [map_kind, wide_kind], (picture, weight_one), flops=7 * work
    )
    hidden, near = call(
        near_edge_kernel,
        [map_kind, wide_kind],
        (edge_distant, edge_chip, weight_one, hidden, near),
        flops=2 * work,
        aliases={3: 0, 4: 1},
    )
    h_chip = swap_chip(hidden)
    h_distant = swap_in_steps(hidden)
    full = pltpu.VMEM((TAPS, CH), F32)
    halves = [pltpu.VMEM((ROWS * HALF, 2 * CH), BF16)] * 2
    parts = [pltpu.VMEM((PART * HALF, 2 * CH), BF16)] * 2
    block_kinds = [shape_of((4, 2, BLOCK, CH), F32), shape_of((4, 2, BLOCK, CH), BF16)]
    begun = call(
        grad_start_kernel,
        shape_of((TAPS, CH), F32),
        (hidden, upstream, c_chip),
        flops=4 * work,
        scratch=halves,
    )
    back = call(
        functools.partial(far_start_kernel, True),
        sum_kind,
        (upstream, c_chip, backward_w),
        flops=4 * work,
    )
    result = call(
        functools.partial(far_start_kernel, False),
        sum_kind,
        (hidden, h_chip, forward_w),
        flops=4 * work,
    )
    masked = [
        call(
            functools.partial(back_end_kernel, i),
            part_kind,
            (back, c_parts[i], backward_w, hidden),
            flops=work,
        )
        for i in range(2)
    ]
    near_part = call(near_part_kernel, shape_of((TAPS, CH), F32), (near, masked[0]), flops=4 * work)
    grad_part = call(
        grad_part_kernel,
        shape_of((3 * CH, CH), F32),
        (hidden, c_parts[0]),
        flops=work,
        scratch=parts,
    )
    keep_one, send_one = call(
        near_end_kernel,
        block_kinds,
        (near_part, near, masked[1]),
        flops=5 * work,
        scratch=[full],
        limit=12,
    )
    keep_two, send_two = call(
        grad_end_kernel,
        block_kinds,
        (begun, grad_part, hidden, c_parts[1]),
        flops=work,
        scratch=[*parts, full],
        limit=12,
    )
    grad_one, grad_two = reduce_grads(keep_one, send_one, keep_two, send_two, factor)
    output = call(conv_end_kernel, map_kind, (result, h_distant, forward_w), flops=2 * work)
    return (output[None], grad_one, grad_two)


def solution(mesh):
    return jax.shard_map(
        on_device,
        mesh=mesh,
        in_specs=(P("dp", "rows", None, None), P("dp", "rows", None, None), P(), P()),
        out_specs=(P("dp", "rows", None, None), P("rows", "dp"), P("rows", "dp")),
        check_vma=False,
    )
```

time: 488 us -> 129 us (0.26); the launches traced: 481 us -> 128 us
  waiting for transfers between devices: 246 us -> 25.2 us
  matrix products: 124 us -> 0 us
  Pallas kernels: 0 us -> 39.5 us
  blocking collectives: 29.6 us -> 0 us
  local copies, waits for them, and re-layouts: 27.4 us -> 7.82 us
  starting transfers between devices: 35.9 us -> 53.8 us
  between operations: 14.3 us -> 0.93 us
    unnamed x8 -> x0, waiting for transfers between devices: 241 us -> none
    dot_general x45 -> x0, matrix products: 124 us -> none  [the longest x18 62.2 us: conv_taps(): product = jnp.dot(window, kernel_block, preferred_element_type=jnp.float32)]
    ppermute x2 -> x25, starting transfers between devices: 3.61 us -> 53.8 us  [the longest x20 47.6 us: send(): return lax.ppermute(block, AXES, pairs_of(move))]
    pallas_call x0 -> x19, Pallas kernels: none -> 39.5 us  [call(): result = run(*args)]
    all_to_all x3 -> x0, starting transfers between devices: 31.7 us -> none  [the longest x1 20.8 us: on_device(): lax.all_to_all(back_cyc.reshape(group_size, row_count // group_size, 1, c...]
    all_to_all x1 -> x0, blocking collectives: 29.6 us -> none  [on_device(): lax.all_to_all(hidden_state.reshape(row_count // group_size, group_size,...]
    ppermute x2 -> x25, waiting for transfers between devices: 0.01 us -> 25.2 us  [the longest x20 25.2 us: send(): return lax.ppermute(block, AXES, pairs_of(move))]
    slice x4 -> x1, local copies, waits for them, and re-layouts: 9.39 us -> 2.43 us  [on_device(): upstream[i * PART:(i + 1) * PART]]
  transfers between devices with their start and end apart: 9 -> 25, of which waited for: 5 -> 7; matrix products, arithmetic and copies ran while one was open for 18% -> 3% of each run, Pallas kernels for 0% -> 31%
where the time goes in v1:
time: 129 us; the launch traced here: 128 us
  starting transfers between devices  53.8 us (42%)
  Pallas kernels  39.5 us (31%)
  waiting for transfers between devices  25.2 us (20%)
  local copies, waits for them, and re-layouts  7.82 us (6%)
    ppermute x20, starting transfers between devices, send(): return lax.ppermute(block, AXES, pairs_of(move))  47.6 us
    pallas_call x19, Pallas kernels, call(): result = run(*args)  39.5 us
    ppermute x20, waiting for transfers between devices, send(): return lax.ppermute(block, AXES, pairs_of(move))  25.2 us
    unnamed x12, local copies, waits for them, and re-layouts  5.39 us
  transfers between devices with their start and end apart: 25, of which 7 were waited for; matrix products, arithmetic and copies ran while one was open for 3% of the time, Pallas kernels for 31%

profile of v1, /device:TPU:0, one launch (start us, length us, event | category | flops | bytes accessed | tf_op | source)
XLA Modules:
  0.0 128.3 jit_solution(9103419312905812526)
XLA Ops:
  0.7 2.4 %slice_bitcast_fusion = (bf16[16,64,384]{2,1,0:T(8,128)(2,1)S(1)}, bf16[16,64,384]{2,1,0:T(8,128)(2,1)}) fusion(bf16[1,32,64,384]{3,2,1,0:T(8,128)(2,1)} %param.5), kind=kLoop, calls=%fused_computation | loop fusion | bytes 3145728 | tf_op jit(solution)/shard_map/slice | solution.py:453
  5.6 4.7 %collective-permute-start.1 = (bf16[4,64,384]{2,1,0:T(8,128)(2,1)S(1)}, bf16[4,64,384]{2,1,0:T(8,128)(2,1)S(1)}, u32[]{:S(2)}, u32[]{:S(2)}) collective-permute-start(bf16[4,64,384]{2,1,0:T(8,128)(2,1)S(1)} %get-tuple-element.72), channel_id=1, source_target_pairs={{0,1},{1,0},{64,65},{65,64},{2,3},{3,2},{66,67},{67,66},{4,5},{5,4... | collective-permute-start | bytes 589832 | tf_op jit(solution)/shard_map/ppermute | solution.py:78
  14.2 7.5 %shard_map.67 = (bf16[32,64,384]{2,1,0:T(8,128)(2,1)S(1)}, bf16[3,40,64,384]{3,2,1,0:T(8,128)(2,1)S(1)}) custom-call(bf16[32,64,384]{2,1,0:T(8,128)(2,1)S(1)} %bitcast.14, bf16[3456,384]{1,0:T(8,128)(2,1)S(1)} %copy-done.1), custom_call_target="tpu_custom_call" | custom-call | flops 4227858432 | bytes 11698176 | tf_op jit(solution)/shard_map/pallas_call | solution.py:39
  23.5 2.6 %shard_map.68 = (bf16[32,64,384]{2,1,0:T(8,128)(2,1)S(1)}, bf16[3,40,64,384]{3,2,1,0:T(8,128)(2,1)S(1)}) custom-call(bf16[4,64,384]{2,1,0:T(8,128)(2,1)S(1)} %collective-permute-done.distant_ref, bf16[4,64,384]{2,1,0:T(8,128)(2,1)S(1)} %collective-permute-done.1.chip_ref, ...), custom_call_target="tpu_custom_call", output_to_operand_aliasing={{0}: (3, {}), {1}: (4, {})} | custom-call | flops 1207959552 | bytes 17989632 | tf_op jit(solution)/shard_map/pallas_call | solution.py:39
  28.7 2.8 %shard_map.72.total_ref = f32[32,64,384]{2,1,0:T(8,128)S(1)} custom-call(bf16[32,64,384]{2,1,0:T(8,128)(2,1)S(1)} %bitcast.12, bf16[32,64,384]{2,1,0:T(8,128)(2,1)S(1)} %collective-permute-done.5.chip_ref, bf16[2304,768]{1,0:T(8,128)(2,1)S(1)} %get-tuple-element.40.w_ref), custom_call_target="tpu_custom_call" | custom-call | flops 2415919104 | bytes 9830400 | tf_op jit(solution)/shard_map/pallas_call | solution.py:39
  33.1 3.8 %shard_map.74.part_ref = f32[3456,384]{1,0:T(8,128)S(1)} custom-call(bf16[3,40,64,384]{3,2,1,0:T(8,128)(2,1)S(1)} %get-tuple-element.39.near_ref, bf16[16,64,384]{2,1,0:T(8,128)(2,1)S(1)} %shard_map.73.masked_ref), custom_call_target="tpu_custom_call" | custom-call | flops 2415919104 | bytes 11993088 | tf_op jit(solution)/shard_map/pallas_call | solution.py:39
  36.9 5.8 %shard_map.76 = (f32[4,2,216,384]{3,2,1,0:T(8,128)S(1)}, bf16[4,2,216,384]{3,2,1,0:T(8,128)(2,1)S(1)}) custom-call(f32[3456,384]{1,0:T(8,128)S(1)} %shard_map.74.part_ref, bf16[3,40,64,384]{3,2,1,0:T(8,128)(2,1)S(1)} %get-tuple-element.39.near_ref, bf16[16,64,384]{2,1,0:T(8,128)(2,1)S(1)} %shard_map.75.masked_ref), custom_call_target="tpu_custom_call" | custom-call | flops 3019898880 | bytes 15974400 | tf_op jit(solution)/shard_map/pallas_call | solution.py:39
  42.7 13.8 %collective-permute-start.8 = (bf16[4,2,216,384]{3,2,1,0:T(8,128)(2,1)S(1)}, bf16[4,2,216,384]{3,2,1,0:T(8,128)(2,1)S(1)}, u32[]{:S(2)}, u32[]{:S(2)}) collective-permute-start(bf16[4,2,216,384]{3,2,1,0:T(8,128)(2,1)S(1)} %get-tuple-element.42), channel_id=1, source_target_pairs={{0,1},{1,0},{64,65},{65,64},{2,3},{3,2},{66,67},{67,66},{4,5},{5,4... | collective-permute-start | bytes 3981320 | tf_op jit(solution)/shard_map/ppermute | solution.py:78
  56.5 2.8 %shard_map.79.begun_ref = f32[3456,384]{1,0:T(8,128)S(1)} custom-call(bf16[32,64,384]{2,1,0:T(8,128)(2,1)S(1)} %get-tuple-element.37.own_ref.hidden_ref, bf16[32,64,384]{2,1,0:T(8,128)(2,1)S(1)} %bitcast.13, bf16[32,64,384]{2,1,0:T(8,128)(2,1)S(1)} %collective-permute-done.5.chip_ref), custom_call_target="tpu_custom_call" | custom-call | flops 2415919104 | bytes 10027008 | tf_op jit(solution)/shard_map/pallas_call | solution.py:39
  62.0 2.5 %collective-permute-start.4 = (bf16[32,64,384]{2,1,0:T(8,128)(2,1)S(1)}, bf16[32,64,384]{2,1,0:T(8,128)(2,1)S(1)}, u32[]{:S(2)}, u32[]{:S(2)}) collective-permute-start(bf16[32,64,384]{2,1,0:T(8,128)(2,1)S(1)} %collective-permute-done.3), channel_id=1, source_target_pairs={{0,3},{1,2},{2,1},{3,0},{4,7},{5,6},{6,5},{7,4},{8,11},{9,10},{10,... | collective-permute-start | bytes 4718600 | tf_op jit(solution)/shard_map/ppermute | solution.py:442
  67.2 2.7 %collective-permute-start.10 = (bf16[2,216,384]{2,1,0:T(8,128)(2,1)S(1)}, bf16[2,216,384]{2,1,0:T(8,128)(2,1)S(1)}, u32[]{:S(2)}, u32[]{:S(2)}) collective-permute-start(bf16[2,216,384]{2,1,0:T(8,128)(2,1)S(1)} %get-tuple-element.45), channel_id=1, source_target_pairs={{0,32},{1,33},{64,96},{65,97},{2,34},{3,35},{66,98},{67,99},{4,36}... | collective-permute-start | bytes 995336 | tf_op jit(solution)/shard_map/ppermute | solution.py:78
  71.6 5.1 %collective-permute-done.9.r1 = bf16[2,216,384]{2,1,0:T(8,128)(2,1)S(1)} collective-permute-done((bf16[2,216,384]{2,1,0:T(8,128)(2,1)S(1)}, bf16[2,216,384]{2,1,0:T(8,128)(2,1)S(1)}, u32[]{:S(2)}, u32[]{:S(2)}) %collective-permute-start.9) | collective-permute-done | bytes 331808 | tf_op jit(solution)/shard_map/ppermute | solution.py:78
  78.2 6.5 %collective-permute-done.10.r2 = bf16[2,216,384]{2,1,0:T(8,128)(2,1)S(1)} collective-permute-done((bf16[2,216,384]{2,1,0:T(8,128)(2,1)S(1)}, bf16[2,216,384]{2,1,0:T(8,128)(2,1)S(1)}, u32[]{:S(2)}, u32[]{:S(2)}) %collective-permute-start.10) | collective-permute-done | bytes 331808 | tf_op jit(solution)/shard_map/ppermute | solution.py:78
  84.8 3.2 %collective-permute-start.17 = (bf16[2,216,384]{2,1,0:T(8,128)(2,1)S(1)}, bf16[2,216,384]{2,1,0:T(8,128)(2,1)S(1)}, u32[]{:S(2)}, u32[]{:S(2)}) collective-permute-start(bf16[2,216,384]{2,1,0:T(8,128)(2,1)S(1)} %get-tuple-element.55), channel_id=1, source_target_pairs={{0,8},{1,9},{64,72},{65,73},{2,10},{3,11},{66,74},{67,75},{4,12},{... | collective-permute-start | bytes 995336 | tf_op jit(solution)/shard_map/ppermute | solution.py:78
  90.7 5.7 %collective-permute-done.17.r2 = bf16[2,216,384]{2,1,0:T(8,128)(2,1)S(1)} collective-permute-done((bf16[2,216,384]{2,1,0:T(8,128)(2,1)S(1)}, bf16[2,216,384]{2,1,0:T(8,128)(2,1)S(1)}, u32[]{:S(2)}, u32[]{:S(2)}) %collective-permute-start.17) | collective-permute-done | bytes 331808 | tf_op jit(solution)/shard_map/ppermute | solution.py:78
  96.4 3.2 %collective-permute-start.13 = (bf16[216,192]{1,0:T(8,128)(2,1)S(1)}, bf16[216,192]{1,0:T(8,128)(2,1)S(1)}, u32[]{:S(2)}, u32[]{:S(2)}) collective-permute-start(bf16[216,192]{1,0:T(8,128)(2,1)S(1)} %get-tuple-element.49), channel_id=1, source_target_pairs={{0,8},{1,9},{64,72},{65,73},{2,10},{3,11},{66,74},{67,75},{4,12},{... | collective-permute-start | bytes 248840 | tf_op jit(solution)/shard_map/ppermute | solution.py:78
  99.6 2.7 %collective-permute-done.18.r3 = bf16[2,216,384]{2,1,0:T(8,128)(2,1)S(1)} collective-permute-done((bf16[2,216,384]{2,1,0:T(8,128)(2,1)S(1)}, bf16[2,216,384]{2,1,0:T(8,128)(2,1)S(1)}, u32[]{:S(2)}, u32[]{:S(2)}) %collective-permute-start.18) | collective-permute-done | bytes 331808 | tf_op jit(solution)/shard_map/ppermute | solution.py:78
  102.4 2.6 %collective-permute-start.14 = (bf16[216,192]{1,0:T(8,128)(2,1)S(1)}, bf16[216,192]{1,0:T(8,128)(2,1)S(1)}, u32[]{:S(2)}, u32[]{:S(2)}) collective-permute-start(bf16[216,192]{1,0:T(8,128)(2,1)S(1)} %get-tuple-element.50), channel_id=1, source_target_pairs={{0,12},{1,13},{64,76},{65,77},{2,14},{3,15},{66,78},{67,79},{4,0},... | collective-permute-start | bytes 248840 | tf_op jit(solution)/shard_map/ppermute | solution.py:78
  106.6 2.7 %collective-permute-start.21 = (bf16[216,192]{1,0:T(8,128)(2,1)S(1)}, bf16[216,192]{1,0:T(8,128)(2,1)S(1)}, u32[]{:S(2)}, u32[]{:S(2)}) collective-permute-start(bf16[216,192]{1,0:T(8,128)(2,1)S(1)} %get-tuple-element.60), channel_id=1, source_target_pairs={{0,48},{1,49},{64,112},{65,113},{2,50},{3,51},{66,114},{67,115},{4... | collective-permute-start | bytes 248840 | tf_op jit(solution)/shard_map/ppermute | solution.py:78
  109.3 2.8 %shard_map.70.total_ref = f32[32,64,384]{2,1,0:T(8,128)S(1)} custom-call(bf16[32,64,384]{2,1,0:T(8,128)(2,1)S(1)} %get-tuple-element.37.own_ref.hidden_ref, bf16[32,64,384]{2,1,0:T(8,128)(2,1)S(1)} %collective-permute-done.2.chip_ref, bf16[2304,768]{1,0:T(8,128)(2,1)S(1)} %get-tuple-element.38.w_ref), custom_call_target="tpu_custom_call" | custom-call | flops 2415919104 | bytes 9830400 | tf_op jit(solution)/shard_map/pallas_call | solution.py:39
  115.2 2.4 %collective-permute-start.22 = (bf16[216,96]{1,0:T(8,128)(2,1)S(1)}, bf16[216,96]{1,0:T(8,128)(2,1)S(1)}, u32[]{:S(2)}, u32[]{:S(2)}) collective-permute-start(bf16[216,96]{1,0:T(8,128)(2,1)S(1)} %get-tuple-element.62), channel_id=1, source_target_pairs={{0,2},{1,3},{64,66},{65,67},{2,0},{3,1},{66,64},{67,65},{4,6},{5,7... | collective-permute-start | bytes 124424 | tf_op jit(solution)/shard_map/ppermute | solution.py:78
  117.6 3.9 %collective-permute-start.23 = (bf16[216,96]{1,0:T(8,128)(2,1)S(1)}, bf16[216,96]{1,0:T(8,128)(2,1)S(1)}, u32[]{:S(2)}, u32[]{:S(2)}) collective-permute-start(bf16[216,96]{1,0:T(8,128)(2,1)S(1)} %get-tuple-element.63), channel_id=1, source_target_pairs={{0,64},{1,65},{64,0},{65,1},{2,66},{3,67},{66,2},{67,3},{4,68},{5,... | collective-permute-start | bytes 124424 | tf_op jit(solution)/shard_map/ppermute | solution.py:78
  121.5 2.7 %shard_map.71 = bf16[32,64,384]{2,1,0:T(8,128)(2,1)} custom-call(f32[32,64,384]{2,1,0:T(8,128)S(1)} %shard_map.70.total_ref, bf16[32,64,384]{2,1,0:T(8,128)(2,1)S(1)} %collective-permute-done.4.distant_ref, bf16[2304,768]{1,0:T(8,128)(2,1)S(1)} %get-tuple-element.38.w_ref), custom_call_target="tpu_custom_call" | custom-call | flops 1207959552 | bytes 9830400 | tf_op jit(solution)/shard_map/pallas_call | solution.py:39
  124.2 2.6 %collective-permute-done.24.r3 = bf16[216,96]{1,0:T(8,128)(2,1)S(1)} collective-permute-done((bf16[216,96]{1,0:T(8,128)(2,1)S(1)}, bf16[216,96]{1,0:T(8,128)(2,1)S(1)}, u32[]{:S(2)}, u32[]{:S(2)}) %collective-permute-start.24) | collective-permute-done | bytes 41504 | tf_op jit(solution)/shard_map/ppermute | solution.py:78
  (59 shorter events, 29.7 us)
Async XLA Ops:
  0.6 28.0 %collective-permute-start.5 = (bf16[32,64,384]{2,1,0:T(8,128)(2,1)}, bf16[32,64,384]{2,1,0:T(8,128)(2,1)S(1)}, u32[]{:S(2)}, u32[]{:S(2)}) collective-permute-start(bf16[32,64,384]{2,1,0:T(8,128)(2,1)} %bitcast.11), channel_id=1, source_target_pairs={{0,1},{1,0},{64,65},{65,64},{2,3},{3,2},{66,67},{67,66},{4,5},{5,4... | collective-permute-start | bytes 4718600 | tf_op jit(solution)/shard_map/ppermute | solution.py:78
  3.2 24.6 %collective-permute-start.6 = (bf16[16,64,384]{2,1,0:T(8,128)(2,1)}, bf16[16,64,384]{2,1,0:T(8,128)(2,1)S(1)}, u32[]{:S(2)}, u32[]{:S(2)}) collective-permute-start(bf16[16,64,384]{2,1,0:T(8,128)(2,1)} %get-tuple-element.71), channel_id=1, source_target_pairs={{1,2},{3,4},{5,6},{7,8},{9,10},{11,12},{13,14},{2,1},{4,3},{6,5},{... | collective-permute-start | bytes 2359304 | tf_op jit(solution)/shard_map/ppermute | solution.py:433
  4.9 17.7 %collective-permute-start = (bf16[4,64,384]{2,1,0:T(8,128)(2,1)S(1)}, bf16[4,64,384]{2,1,0:T(8,128)(2,1)S(1)}, u32[]{:S(2)}, u32[]{:S(2)}) collective-permute-start(bf16[4,64,384]{2,1,0:T(8,128)(2,1)S(1)} %get-tuple-element.73), channel_id=1, source_target_pairs={{1,2},{3,4},{5,6},{7,8},{9,10},{11,12},{13,14},{2,1},{4,3},{6,5},{... | collective-permute-start | bytes 589832 | tf_op jit(solution)/shard_map/ppermute | solution.py:433
  5.6 17.1 %collective-permute-start.1 = (bf16[4,64,384]{2,1,0:T(8,128)(2,1)S(1)}, bf16[4,64,384]{2,1,0:T(8,128)(2,1)S(1)}, u32[]{:S(2)}, u32[]{:S(2)}) collective-permute-start(bf16[4,64,384]{2,1,0:T(8,128)(2,1)S(1)} %get-tuple-element.72), channel_id=1, source_target_pairs={{0,1},{1,0},{64,65},{65,64},{2,3},{3,2},{66,67},{67,66},{4,5},{5,4... | collective-permute-start | bytes 589832 | tf_op jit(solution)/shard_map/ppermute | solution.py:78
  10.4 21.9 %collective-permute-start.7 = (bf16[16,64,384]{2,1,0:T(8,128)(2,1)S(1)}, bf16[16,64,384]{2,1,0:T(8,128)(2,1)S(1)}, u32[]{:S(2)}, u32[]{:S(2)}) collective-permute-start(bf16[16,64,384]{2,1,0:T(8,128)(2,1)S(1)} %get-tuple-element.70), channel_id=1, source_target_pairs={{1,2},{3,4},{5,6},{7,8},{9,10},{11,12},{13,14},{2,1},{4,3},{6,5},{... | collective-permute-start | bytes 2359304 | tf_op jit(solution)/shard_map/ppermute | solution.py:433
  26.2 35.8 %collective-permute-start.3 = (bf16[32,64,384]{2,1,0:T(8,128)(2,1)S(1)}, bf16[32,64,384]{2,1,0:T(8,128)(2,1)S(1)}, u32[]{:S(2)}, u32[]{:S(2)}) collective-permute-start(bf16[32,64,384]{2,1,0:T(8,128)(2,1)S(1)} %get-tuple-element.37.own_ref.hidden_ref), channel_id=1, source_target_pairs={{1,1},{2,2},{5,5},{6,6},{9,9},{10,10},{13,13},{14,14},{3,7},{4,0},... | collective-permute-start | bytes 4718600 | tf_op jit(solution)/shard_map/ppermute | solution.py:441
  42.7 21.7 %collective-permute-start.8 = (bf16[4,2,216,384]{3,2,1,0:T(8,128)(2,1)S(1)}, bf16[4,2,216,384]{3,2,1,0:T(8,128)(2,1)S(1)}, u32[]{:S(2)}, u32[]{:S(2)}) collective-permute-start(bf16[4,2,216,384]{3,2,1,0:T(8,128)(2,1)S(1)} %get-tuple-element.42), channel_id=1, source_target_pairs={{0,1},{1,0},{64,65},{65,64},{2,3},{3,2},{66,67},{67,66},{4,5},{5,4... | collective-permute-start | bytes 3981320 | tf_op jit(solution)/shard_map/ppermute | solution.py:78
  61.4 8.5 %collective-permute-start.15 = (bf16[4,2,216,384]{3,2,1,0:T(8,128)(2,1)S(1)}, bf16[4,2,216,384]{3,2,1,0:T(8,128)(2,1)S(1)}, u32[]{:S(2)}, u32[]{:S(2)}) collective-permute-start(bf16[4,2,216,384]{3,2,1,0:T(8,128)(2,1)S(1)} %get-tuple-element.52), channel_id=1, source_target_pairs={{0,1},{1,0},{64,65},{65,64},{2,3},{3,2},{66,67},{67,66},{4,5},{5,4... | collective-permute-start | bytes 3981320 | tf_op jit(solution)/shard_map/ppermute | solution.py:78
  61.5 44.2 %collective-permute-start.2 = (bf16[32,64,384]{2,1,0:T(8,128)(2,1)S(1)}, bf16[32,64,384]{2,1,0:T(8,128)(2,1)S(1)}, u32[]{:S(2)}, u32[]{:S(2)}) collective-permute-start(bf16[32,64,384]{2,1,0:T(8,128)(2,1)S(1)} %get-tuple-element.37.own_ref.hidden_ref), channel_id=1, source_target_pairs={{0,1},{1,0},{64,65},{65,64},{2,3},{3,2},{66,67},{67,66},{4,5},{5,4... | collective-permute-start | bytes 4718600 | tf_op jit(solution)/shard_map/ppermute | solution.py:78
  62.0 59.5 %collective-permute-start.4 = (bf16[32,64,384]{2,1,0:T(8,128)(2,1)S(1)}, bf16[32,64,384]{2,1,0:T(8,128)(2,1)S(1)}, u32[]{:S(2)}, u32[]{:S(2)}) collective-permute-start(bf16[32,64,384]{2,1,0:T(8,128)(2,1)S(1)} %collective-permute-done.3), channel_id=1, source_target_pairs={{0,3},{1,2},{2,1},{3,0},{4,7},{5,6},{6,5},{7,4},{8,11},{9,10},{10,... | collective-permute-start | bytes 4718600 | tf_op jit(solution)/shard_map/ppermute | solution.py:442
  65.6 11.1 %collective-permute-start.9 = (bf16[2,216,384]{2,1,0:T(8,128)(2,1)S(1)}, bf16[2,216,384]{2,1,0:T(8,128)(2,1)S(1)}, u32[]{:S(2)}, u32[]{:S(2)}) collective-permute-start(bf16[2,216,384]{2,1,0:T(8,128)(2,1)S(1)} %get-tuple-element.44), channel_id=1, source_target_pairs={{0,16},{1,17},{64,80},{65,81},{2,18},{3,19},{66,82},{67,83},{4,20}... | collective-permute-start | bytes 995336 | tf_op jit(solution)/shard_map/ppermute | solution.py:78
  67.2 17.6 %collective-permute-start.10 = (bf16[2,216,384]{2,1,0:T(8,128)(2,1)S(1)}, bf16[2,216,384]{2,1,0:T(8,128)(2,1)S(1)}, u32[]{:S(2)}, u32[]{:S(2)}) collective-permute-start(bf16[2,216,384]{2,1,0:T(8,128)(2,1)S(1)} %get-tuple-element.45), channel_id=1, source_target_pairs={{0,32},{1,33},{64,96},{65,97},{2,34},{3,35},{66,98},{67,99},{4,36}... | collective-permute-start | bytes 995336 | tf_op jit(solution)/shard_map/ppermute | solution.py:78
  69.9 18.1 %collective-permute-start.11 = (bf16[2,216,384]{2,1,0:T(8,128)(2,1)S(1)}, bf16[2,216,384]{2,1,0:T(8,128)(2,1)S(1)}, u32[]{:S(2)}, u32[]{:S(2)}) collective-permute-start(bf16[2,216,384]{2,1,0:T(8,128)(2,1)S(1)} %get-tuple-element.46), channel_id=1, source_target_pairs={{0,48},{1,49},{64,112},{65,113},{2,50},{3,51},{66,114},{67,115},{4... | collective-permute-start | bytes 995336 | tf_op jit(solution)/shard_map/ppermute | solution.py:78
  76.7 13.0 %collective-permute-start.16 = (bf16[2,216,384]{2,1,0:T(8,128)(2,1)S(1)}, bf16[2,216,384]{2,1,0:T(8,128)(2,1)S(1)}, u32[]{:S(2)}, u32[]{:S(2)}) collective-permute-start(bf16[2,216,384]{2,1,0:T(8,128)(2,1)S(1)} %get-tuple-element.54), channel_id=1, source_target_pairs={{0,4},{1,5},{64,68},{65,69},{2,6},{3,7},{66,70},{67,71},{4,8},{5,9... | collective-permute-start | bytes 995336 | tf_op jit(solution)/shard_map/ppermute | solution.py:78
  84.8 11.6 %collective-permute-start.17 = (bf16[2,216,384]{2,1,0:T(8,128)(2,1)S(1)}, bf16[2,216,384]{2,1,0:T(8,128)(2,1)S(1)}, u32[]{:S(2)}, u32[]{:S(2)}) collective-permute-start(bf16[2,216,384]{2,1,0:T(8,128)(2,1)S(1)} %get-tuple-element.55), channel_id=1, source_target_pairs={{0,8},{1,9},{64,72},{65,73},{2,10},{3,11},{66,74},{67,75},{4,12},{... | collective-permute-start | bytes 995336 | tf_op jit(solution)/shard_map/ppermute | solution.py:78
  88.0 14.4 %collective-permute-start.18 = (bf16[2,216,384]{2,1,0:T(8,128)(2,1)S(1)}, bf16[2,216,384]{2,1,0:T(8,128)(2,1)S(1)}, u32[]{:S(2)}, u32[]{:S(2)}) collective-permute-start(bf16[2,216,384]{2,1,0:T(8,128)(2,1)S(1)} %get-tuple-element.56), channel_id=1, source_target_pairs={{0,12},{1,13},{64,76},{65,77},{2,14},{3,15},{66,78},{67,79},{4,0},... | collective-permute-start | bytes 995336 | tf_op jit(solution)/shard_map/ppermute | solution.py:78
  89.6 16.1 %collective-permute-start.12 = (bf16[216,192]{1,0:T(8,128)(2,1)S(1)}, bf16[216,192]{1,0:T(8,128)(2,1)S(1)}, u32[]{:S(2)}, u32[]{:S(2)}) collective-permute-start(bf16[216,192]{1,0:T(8,128)(2,1)S(1)} %get-tuple-element.48), channel_id=1, source_target_pairs={{0,4},{1,5},{64,68},{65,69},{2,6},{3,7},{66,70},{67,71},{4,8},{5,9... | collective-permute-start | bytes 248840 | tf_op jit(solution)/shard_map/ppermute | solution.py:78
  96.4 10.2 %collective-permute-start.13 = (bf16[216,192]{1,0:T(8,128)(2,1)S(1)}, bf16[216,192]{1,0:T(8,128)(2,1)S(1)}, u32[]{:S(2)}, u32[]{:S(2)}) collective-permute-start(bf16[216,192]{1,0:T(8,128)(2,1)S(1)} %get-tuple-element.49), channel_id=1, source_target_pairs={{0,8},{1,9},{64,72},{65,73},{2,10},{3,11},{66,74},{67,75},{4,12},{... | collective-permute-start | bytes 248840 | tf_op jit(solution)/shard_map/ppermute | solution.py:78
  102.4 9.7 %collective-permute-start.14 = (bf16[216,192]{1,0:T(8,128)(2,1)S(1)}, bf16[216,192]{1,0:T(8,128)(2,1)S(1)}, u32[]{:S(2)}, u32[]{:S(2)}) collective-permute-start(bf16[216,192]{1,0:T(8,128)(2,1)S(1)} %get-tuple-element.50), channel_id=1, source_target_pairs={{0,12},{1,13},{64,76},{65,77},{2,14},{3,15},{66,78},{67,79},{4,0},... | collective-permute-start | bytes 248840 | tf_op jit(solution)/shard_map/ppermute | solution.py:78
  105.6 8.3 %collective-permute-start.19 = (bf16[216,192]{1,0:T(8,128)(2,1)S(1)}, bf16[216,192]{1,0:T(8,128)(2,1)S(1)}, u32[]{:S(2)}, u32[]{:S(2)}) collective-permute-start(bf16[216,192]{1,0:T(8,128)(2,1)S(1)} %get-tuple-element.58), channel_id=1, source_target_pairs={{0,16},{1,17},{64,80},{65,81},{2,18},{3,19},{66,82},{67,83},{4,20}... | collective-permute-start | bytes 248840 | tf_op jit(solution)/shard_map/ppermute | solution.py:78
  105.7 8.3 %collective-permute-start.20 = (bf16[216,192]{1,0:T(8,128)(2,1)S(1)}, bf16[216,192]{1,0:T(8,128)(2,1)S(1)}, u32[]{:S(2)}, u32[]{:S(2)}) collective-permute-start(bf16[216,192]{1,0:T(8,128)(2,1)S(1)} %get-tuple-element.59), channel_id=1, source_target_pairs={{0,32},{1,33},{64,96},{65,97},{2,34},{3,35},{66,98},{67,99},{4,36}... | collective-permute-start | bytes 248840 | tf_op jit(solution)/shard_map/ppermute | solution.py:78
  106.6 8.0 %collective-permute-start.21 = (bf16[216,192]{1,0:T(8,128)(2,1)S(1)}, bf16[216,192]{1,0:T(8,128)(2,1)S(1)}, u32[]{:S(2)}, u32[]{:S(2)}) collective-permute-start(bf16[216,192]{1,0:T(8,128)(2,1)S(1)} %get-tuple-element.60), channel_id=1, source_target_pairs={{0,48},{1,49},{64,112},{65,113},{2,50},{3,51},{66,114},{67,115},{4... | collective-permute-start | bytes 248840 | tf_op jit(solution)/shard_map/ppermute | solution.py:78
  115.2 9.1 %collective-permute-start.22 = (bf16[216,96]{1,0:T(8,128)(2,1)S(1)}, bf16[216,96]{1,0:T(8,128)(2,1)S(1)}, u32[]{:S(2)}, u32[]{:S(2)}) collective-permute-start(bf16[216,96]{1,0:T(8,128)(2,1)S(1)} %get-tuple-element.62), channel_id=1, source_target_pairs={{0,2},{1,3},{64,66},{65,67},{2,0},{3,1},{66,64},{67,65},{4,6},{5,7... | collective-permute-start | bytes 124424 | tf_op jit(solution)/shard_map/ppermute | solution.py:78
  117.6 6.6 %collective-permute-start.23 = (bf16[216,96]{1,0:T(8,128)(2,1)S(1)}, bf16[216,96]{1,0:T(8,128)(2,1)S(1)}, u32[]{:S(2)}, u32[]{:S(2)}) collective-permute-start(bf16[216,96]{1,0:T(8,128)(2,1)S(1)} %get-tuple-element.63), channel_id=1, source_target_pairs={{0,64},{1,65},{64,0},{65,1},{2,66},{3,67},{66,2},{67,3},{4,68},{5,... | collective-permute-start | bytes 124424 | tf_op jit(solution)/shard_map/ppermute | solution.py:78
  (6 other events, 20.3 us)

commit v2 on v1

--- a/solution.py
+++ b/solution.py
@@ -18,18 +18,20 @@
 TAPS = 9 * CH
 BLOCK = 216
 SLIM = 48
+TALL = 112
 WHOLE = pl.BlockSpec(memory_space=pltpu.VMEM)
+PARTS = ((0, 20), (20, 12))
 AXES = ("dp", "rows")
 
 
-def call(kernel, outs, args, flops=0, scratch=(), limit=8, aliases=None):
+def call(kernel, outs, args, flops=0, scratch=(), limit=8, aliases=None, where=None):
     single = not isinstance(outs, (list, tuple))
     shapes = [outs] if single else list(outs)
     moved = sum(a.size * a.dtype.itemsize for a in list(args) + shapes)
     run = pl.pallas_call(
         kernel,
         out_shape=shapes,
-        in_specs=[WHOLE] * len(args),
+        in_specs=where or [WHOLE] * len(args),
         out_specs=[WHOLE] * len(shapes),
         scratch_shapes=list(scratch),
         input_output_aliases=aliases or {},
@@ -110,10 +112,15 @@
     )
 
 
-def near_mid_kernel(own_ref, w_ref, hidden_ref, near_ref):
+def near_mid_kernel(own_ref, far_ref, hidden_ref, near_ref, w_ref, sem):
+    copy = pltpu.make_async_copy(far_ref, w_ref, sem)
+    copy.start()
+
     @pl.loop(0, ROWS // 4)
     def _(i):
         shifted_store(near_ref, 4 + i * 4, own_ref[pl.ds(i * 4, 4)])
+
+    copy.wait()
 
     @pl.loop(0, 3)
     def _(m):
@@ -159,9 +166,6 @@
             ].reshape(chunk, HALF, CH)
 
 
-PART = ROWS // 2
-
-
 def distant_part(distant_ref, w_ref, at, first, chunk):
     return matmul(side_rows(distant_ref, first, chunk), block_of(w_ref, at))
 
@@ -179,24 +183,27 @@
             out_ref[where] = (total_ref[where] + part).astype(BF16)
 
 
-def back_end_kernel(index, total_ref, distant_ref, w_ref, hidden_ref, out_ref):
-    core = place()[4]
-    total = distant_part(distant_ref, w_ref, 2 - 2 * core, 0, PART)
+def back_end_kernel(first, count, total_ref, distant_ref, w_ref, hidden_ref, out_ref):
+    core = place()[4]
+    total = distant_part(distant_ref, w_ref, 2 - 2 * core, 0, count)
     for side in range(2):
         cols = slice(side * HALF, (side + 1) * HALF)
-        where = (slice(index * PART, (index + 1) * PART), cols)
-        part = total[:, side * CH : (side + 1) * CH].reshape(PART, HALF, CH)
+        where = (slice(first, first + count), cols)
+        part = total[:, side * CH : (side + 1) * CH].reshape(count, HALF, CH)
         value = (total_ref[where] + part).astype(BF16)
         out_ref[:, cols] = jnp.where(hidden_ref[where] > 0, value, jnp.zeros_like(value))
 
 
-def split_cores(full_ref, keep_ref, send_ref):
-    core = place()[4]
-    for j in range(8):
-        mine = full_ref[pl.ds(pl.multiple_of((2 * j + core) * BLOCK, 8), BLOCK)]
-        other = full_ref[pl.ds(pl.multiple_of((2 * j + 1 - core) * BLOCK, 8), BLOCK)]
-        keep_ref[j // 2, j % 2] = mine
-        send_ref[j // 2, j % 2] = other.astype(BF16)
+def block_at(full_ref, y, low, core, at=0, count=BLOCK):
+    first = pl.multiple_of((4 * y + 2 * low + core) * BLOCK + at, 8)
+    return full_ref[pl.ds(first, count)]
+
+
+def fill_send(full_ref, send_ref):
+    core = place()[4]
+    for y in range(4):
+        for low in range(2):
+            send_ref[y, low] = block_at(full_ref, y, low, 1 - core).astype(BF16)
 
 
 def outer(left, right):
@@ -231,58 +238,61 @@
 
 
 def fill_part(ref, first, out_ref):
+    count = out_ref.shape[0] // HALF
     for side in range(2):
         out_ref[:, side * CH : (side + 1) * CH] = ref[
-            first : first + PART, side * HALF : (side + 1) * HALF
-        ].reshape(PART * HALF, CH)
-
-
-def grad_part_kernel(hidden_ref, distant_ref, part_ref, h_ref, c_ref):
-    fill_part(hidden_ref, 0, h_ref)
+            first : first + count, side * HALF : (side + 1) * HALF
+        ].reshape(count * HALF, CH)
+
+
+def grad_part_kernel(first, hidden_ref, distant_ref, begun_ref, full_ref, *refs):
+    core = place()[4]
+    h_ref, c_ref = refs[-2:]
+    fill_part(hidden_ref, first, h_ref)
     fill_part(distant_ref, 0, c_ref)
-    outer_taps(h_ref, c_ref, part_ref)
-
-
-def grad_end_kernel(
-    begun_ref, part_ref, hidden_ref, distant_ref, keep_ref, send_ref, h_ref, c_ref, full_ref
-):
-    core = place()[4]
-    fill_part(hidden_ref, PART, h_ref)
-    fill_part(distant_ref, 0, c_ref)
+    grad = outer(h_ref[...], c_ref[...])
     target = taps_at(full_ref, 2 - 2 * core)
-    outer_taps(h_ref, c_ref, target)
-    target[...] = target[...] + part_ref[...]
-    for at in (1, 2 * core):
-        taps_at(full_ref, at)[...] = taps_at(begun_ref, at)[...]
-    split_cores(full_ref, keep_ref, send_ref)
-
-
-def near_window(near_ref, index, a, b):
-    first = 4 * a + index * PART
-    return near_ref[b, first : first + PART].reshape(PART * COLS, CH)
-
-
-def near_part_kernel(near_ref, masked_ref, part_ref):
-    target = masked_ref[...].reshape(PART * COLS, CH)
+    terms = (grad[:CH, CH:], grad[:CH, :CH] + grad[CH:, CH:], grad[CH:, :CH])
+    for b, term in enumerate(terms):
+        where = slice(b * CH, (b + 1) * CH)
+        target[where] = target[where] + term if first else term
+    if len(refs) == 3:
+        fill_send(full_ref, refs[0])
+
+
+def near_part_kernel(first, count, near_ref, masked_ref, *refs):
+    if first:
+        refs = refs[1:]
+    full_ref = refs[0]
+    target = masked_ref[...].reshape(count * COLS, CH)
     for a in range(3):
         for b in range(3):
-            part_ref[pl.ds((3 * a + b) * CH, CH)] = outer(near_window(near_ref, 0, a, b), target)
-
-
-def near_end_kernel(part_ref, near_ref, masked_ref, keep_ref, send_ref, full_ref):
-    target = masked_ref[...].reshape(PART * COLS, CH)
-    for a in range(3):
-        for b in range(3):
+            start = 4 * a + first
+            window = near_ref[b, start : start + count].reshape(count * COLS, CH)
             where = pl.ds((3 * a + b) * CH, CH)
-            full_ref[where] = part_ref[where] + outer(near_window(near_ref, 1, a, b), target)
-    split_cores(full_ref, keep_ref, send_ref)
+            term = outer(window, target)
+            full_ref[where] = full_ref[where] + term if first else term
+    if len(refs) == 2:
+        fill_send(full_ref, refs[1])
 
 
 BANDS = tuple((at, min(48, BLOCK - at)) for at in range(0, BLOCK, 48))
 
 
-def one_first_kernel(keep_ref, got_ref, own_ref, p1, p2, p3, hold_ref):
-    x = place()[0]
+def partners(spot, core):
+    return spot ^ (1 + 2 * core), spot ^ (3 - 2 * core), spot ^ 2
+
+
+def hand_out(piece, spot, core, own_ref, other_ref, send_ref):
+    near, later, across = partners(spot, core)
+    own_ref[...] = piece(spot)
+    other_ref[...] = piece(later)
+    send_ref[0] = piece(near).astype(BF16)
+    send_ref[1] = piece(across).astype(BF16)
+
+
+def one_first_kernel(full_ref, got_ref, own_ref, other_ref, send_ref, hold_ref):
+    x, _, _, _, core = place()
     for at, count in BANDS:
         band = slice(at, at + count)
         lane = lax.broadcasted_iota(jnp.int32, (count, CH), 1)
@@ -290,39 +300,49 @@
         for low in range(2):
             turned = []
             for y in range(4):
-                total = keep_ref[y, low, band] + got_ref[y, low, band].astype(F32)
+                total = block_at(full_ref, y, low, core, at, count)
+                total = total + got_ref[y, low, band].astype(F32)
                 turned.append(pltpu.roll(total, SLIM * y, 1) if y else total)
             for q in range(4):
                 part = turned[(3 - q) % 4]
                 for r in (2, 1, 0):
                     part = jnp.where(lane < (r + 1) * SLIM, turned[(r - q) % 4], part)
                 hold_ref[q, low, band] = part
-    own_ref[...] = hold_ref[x]
-    for k, ref in enumerate((p1, p2, p3)):
-        ref[...] = hold_ref[lax.rem(x + k + 1, 4)].astype(BF16)
-
-
-def two_first_kernel(keep_ref, got_ref, *refs):
-    y = place()[1]
-    for k, ref in enumerate(refs):
-        at = lax.rem(y + k, 4)
-        ref[...] = (keep_ref[at] + got_ref[at].astype(F32)).astype(ref.dtype)
-
-
-def second_kernel(turned, kept_ref, r1, r2, r3, own_ref, p1, p2, p3, hold_ref):
+    hand_out(lambda q: hold_ref[q], x, core, own_ref, other_ref, send_ref)
+
+
+def two_first_kernel(full_ref, got_ref, own_ref, other_ref, send_ref):
+    _, y, _, _, core = place()
+    near, later, across = partners(y, core)
+    spots = ((own_ref, y), (other_ref, later), (send_ref.at[0], near), (send_ref.at[1], across))
+    for ref, at in spots:
+        for low in range(2):
+            total = block_at(full_ref, at, low, core) + got_ref[at, low].astype(F32)
+            ref[low] = total.astype(ref.dtype)
+
+
+def middle_kernel(other_ref, got_ref, out_ref):
+    out_ref[...] = (other_ref[...] + got_ref[1].astype(F32)).astype(BF16)
+
+
+PACKS = ((0, 48), (48, 48), (96, 16), (112, 48), (160, 48), (208, 8))
+
+
+def second_kernel(turned, kept_ref, got_ref, last_ref, own_ref, p1, p2, p3, hold_ref):
     x, y = place()[:2]
     base = x + y if turned else x
-    for at, count in BANDS:
+    for at, count in PACKS:
         band = slice(at, at + count)
+        right = at >= TALL
+        rows = slice(at - TALL, at - TALL + count) if right else band
         for low in range(2):
-            total = kept_ref[low, band]
-            for r in (r1, r2, r3):
-                total = total + r[low, band].astype(F32)
+            total = kept_ref[low, band] + got_ref[0, low, band].astype(F32)
+            total = total + last_ref[low, band].astype(F32)
             for q in range(4):
                 for side in range(2):
                     start = side * 4 * SLIM + q * SLIM
-                    to = (2 * low + side) * SLIM
-                    hold_ref[q, band, to : to + SLIM] = total[:, start : start + SLIM]
+                    to = (4 * right + 2 * low + side) * SLIM
+                    hold_ref[q, rows, to : to + SLIM] = total[:, start : start + SLIM]
     own_ref[...] = hold_ref[lax.rem(base, 4)]
     for k, ref in enumerate((p1, p2, p3)):
         ref[...] = hold_ref[lax.rem(base + k + 1, 4)].astype(BF16)
@@ -339,7 +359,9 @@
         for l in range(2):
             for side in range(2):
                 at = (2 * l + side) * SLIM
-                hold_ref[g, l, side] = total[:, at : at + SLIM]
+                hold_ref[g, l, side, 0:TALL] = total[:, at : at + SLIM]
+                at = at + 4 * SLIM
+                hold_ref[g, l, side, TALL:BLOCK] = total[: BLOCK - TALL, at : at + SLIM]
         here = high if g else lax.rem(high + lax.div(x + y, 4), 2)
         spots = ((low, here), (1 - low, here), (low, 1 - here), (1 - low, 1 - here))
         for ref, (l, side) in zip((own_ref, p1, p2, p3), spots):
@@ -351,8 +373,13 @@
     for ref in (r1, r2, r3):
         total = total + ref[...].astype(F32)
     total = total * factor
-    one_ref[...] = total[:, 0:SLIM]
-    two_ref[...] = total[:, SLIM : 2 * SLIM]
+    total = total.T
+    one_ref[...] = total[0:SLIM]
+    two_ref[...] = total[SLIM : 2 * SLIM]
+
+
+def parcels_of(dims):
+    return [shape_of(dims, F32), shape_of(dims, F32), shape_of((2, *dims), BF16)]
 
 
 def pieces_of(dims):
@@ -363,24 +390,30 @@
     return send(block, lambda x, y, l, h, c: (x, y, l, h, 1 - c))
 
 
-def over_x(pieces):
-    own, *pieces = pieces
-    result = [own]
-    for k, piece in enumerate(pieces):
-        result.append(send(piece, lambda x, y, l, h, c: (x + k + 1, y, l, h, c)))
-    return result
-
-
-def over_y(pieces):
-    own, *pieces = pieces
-    result = [own]
-    for k, piece in enumerate(pieces):
-        result.append(send(piece, lambda x, y, l, h, c: (x, y + k + 1, l, h, c)))
-    return result
+def along(axis, step):
+    def move(x, y, l, h, c):
+        flip = (1 + 2 * c, 3 - 2 * c)[step]
+        z = l + 2 * h
+        if axis == "x":
+            x = x ^ flip
+        elif axis == "y":
+            y = y ^ flip
+        else:
+            z = z ^ flip
+        return x, y, z % 2, z // 2, c
+
+    return move
+
+
+def exchange(pieces, axis):
+    own, other, parcel = pieces
+    got = send(parcel, along(axis, 0))
+    parcel = call(middle_kernel, shape_of(own.shape, BF16), (other, got))
+    return own, got, send(parcel, along(axis, 1))
 
 
 def second_stage(turned, held):
-    dims = (BLOCK, 4 * SLIM)
+    dims = (TALL, 8 * SLIM)
     return call(
         functools.partial(second_kernel, turned),
         pieces_of(dims),
@@ -389,21 +422,32 @@
     )
 
 
-def reduce_grads(keep_one, send_one, keep_two, send_two, factor):
+def over(pieces, axis):
+    own, *pieces = pieces
+    result = [own]
+    for k, piece in enumerate(pieces):
+        if axis == "x":
+            result.append(send(piece, lambda x, y, l, h, c: (x + k + 1, y, l, h, c)))
+        else:
+            result.append(send(piece, lambda x, y, l, h, c: (x, y + k + 1, l, h, c)))
+    return result
+
+
+def reduce_grads(full_one, send_one, full_two, send_two, factor):
     got_one = swap_core(send_one)
     got_two = swap_core(send_two)
     dims = (2, BLOCK, CH)
     one = call(
         one_first_kernel,
-        pieces_of(dims),
-        (keep_one, got_one),
+        parcels_of(dims),
+        (full_one, got_one),
         scratch=[pltpu.VMEM((4, *dims), F32)],
     )
-    two = call(two_first_kernel, pieces_of(dims), (keep_two, got_two))
-    one = second_stage(True, over_x(one))
-    two = second_stage(False, over_y(two))
-    one = over_y(one)
-    two = over_x(two)
+    two = call(two_first_kernel, parcels_of(dims), (full_two, got_two))
+    one = second_stage(True, exchange(one, "x"))
+    two = second_stage(False, exchange(two, "y"))
+    one = over(one, "y")
+    two = over(two, "x")
     dims = (BLOCK, 2 * SLIM)
     own, *pieces = call(
         third_kernel,
@@ -419,8 +463,9 @@
     got = []
     for piece, move in zip(pieces, moves):
         got.append(send(piece, move))
-    kind = shape_of((BLOCK, SLIM), F32)
-    return call(functools.partial(last_kernel, factor), [kind, kind], (own, *got))
+    kind = shape_of((SLIM, BLOCK), F32)
+    one, two = call(functools.partial(last_kernel, factor), [kind, kind], (own, *got))
+    return one.T, two.T
 
 
 def swap_chip(block):
@@ -450,17 +495,22 @@
     first_core = lax.rem(lax.axis_index("rows"), 2) == 0
     head, tail = picture[:4], picture[-4:]
     edge_distant = swap_distant(jnp.where(first_core, head, tail))
-    c_parts = [swap_distant(upstream[i * PART : (i + 1) * PART]) for i in range(2)]
     edge_chip = swap_chip(jnp.where(first_core, tail, head))
+    part_kinds = [shape_of((count, COLS, CH), BF16) for _, count in PARTS]
+    c_parts = [swap_distant(upstream[first : first + count]) for first, count in PARTS]
     c_chip = swap_chip(upstream)
     kind = shape_of((6 * CH, 2 * CH), BF16)
     forward_w, backward_w = call(weight_kernel, [kind, kind], (weight_two,))
     map_kind = shape_of((ROWS, COLS, CH), BF16)
-    part_kind = shape_of((PART, COLS, CH), BF16)
     sum_kind = shape_of((ROWS, COLS, CH), F32)
     wide_kind = shape_of((3, ROWS + 8, COLS, CH), BF16)
-    hidden, near = call(
-        near_mid_kernel, [map_kind, wide_kind], (picture, weight_one), flops=7 * work
+    hidden, near, weight_one = call(
+        near_mid_kernel,
+        [map_kind, wide_kind, shape_of((TAPS, CH), BF16)],
+        (picture, pltpu.with_memory_space_constraint(weight_one, pltpu.HBM)),
+        flops=7 * work,
+        scratch=[pltpu.SemaphoreType.DMA],
+        where=[WHOLE, pl.BlockSpec(memory_space=pltpu.HBM)],
     )
     hidden, near = call(
         near_edge_kernel,
@@ -471,10 +521,9 @@
     )
     h_chip = swap_chip(hidden)
     h_distant = swap_in_steps(hidden)
-    full = pltpu.VMEM((TAPS, CH), F32)
     halves = [pltpu.VMEM((ROWS * HALF, 2 * CH), BF16)] * 2
-    parts = [pltpu.VMEM((PART * HALF, 2 * CH), BF16)] * 2
-    block_kinds = [shape_of((4, 2, BLOCK, CH), F32), shape_of((4, 2, BLOCK, CH), BF16)]
+    full_kind = shape_of((TAPS, CH), F32)
+    send_kind = shape_of((4, 2, BLOCK, CH), BF16)
     begun = call(
         grad_start_kernel,
         shape_of((TAPS, CH), F32),
@@ -494,40 +543,35 @@
         (hidden, h_chip, forward_w),
         flops=4 * work,
     )
-    masked = [
-        call(
-            functools.partial(back_end_kernel, i),
-            part_kind,
+    last = len(PARTS) - 1
+    full_one, full_two = None, begun
+    for i, (first, count) in enumerate(PARTS):
+        share = count * work // ROWS
+        masked = call(
+            functools.partial(back_end_kernel, first, count),
+            part_kinds[i],
             (back, c_parts[i], backward_w, hidden),
-            flops=work,
+            flops=2 * share,
         )
-        for i in range(2)
-    ]
-    near_part = call(near_part_kernel, shape_of((TAPS, CH), F32), (near, masked[0]), flops=4 * work)
-    grad_part = call(
-        grad_part_kernel,
-        shape_of((3 * CH, CH), F32),
-        (hidden, c_parts[0]),
-        flops=work,
-        scratch=parts,
-    )
-    keep_one, send_one = call(
-        near_end_kernel,
-        block_kinds,
-        (near_part, near, masked[1]),
-        flops=5 * work,
-        scratch=[full],
-        limit=12,
-    )
-    keep_two, send_two = call(
-        grad_end_kernel,
-        block_kinds,
-        (begun, grad_part, hidden, c_parts[1]),
-        flops=work,
-        scratch=[*parts, full],
-        limit=12,
-    )
-    grad_one, grad_two = reduce_grads(keep_one, send_one, keep_two, send_two, factor)
+        kinds = [full_kind, send_kind] if i == last else [full_kind]
+        near_out = call(
+            functools.partial(near_part_kernel, first, count),
+            kinds,
+            (near, masked) if i == 0 else (near, masked, full_one),
+            flops=9 * share,
+            aliases={} if i == 0 else {2: 0},
+        )
+        full_one = near_out[0]
+        grad_out = call(
+            functools.partial(grad_part_kernel, first),
+            kinds,
+            (hidden, c_parts[i], full_two),
+            flops=2 * share,
+            scratch=[pltpu.VMEM((count * HALF, 2 * CH), BF16)] * 2,
+            aliases={2: 0},
+        )
+        full_two = grad_out[0]
+    grad_one, grad_two = reduce_grads(full_one, near_out[1], full_two, grad_out[1], factor)
     output = call(conv_end_kernel, map_kind, (result, h_distant, forward_w), flops=2 * work)
     return (output[None], grad_one, grad_two)
 

time: 129 us -> 106 us (0.82)
  waiting for transfers between devices: 25.2 us -> 14.4 us
  local copies, waits for them, and re-layouts: 7.82 us -> 1.38 us
  starting transfers between devices: 53.8 us -> 47.6 us
    ppermute x20 -> x18, waiting for transfers between devices: 25.2 us -> 14.4 us  [send(): return lax.ppermute(block, AXES, pairs_of(move))]
    ppermute x20 -> x18, starting transfers between devices: 47.6 us -> 41.5 us  [send(): return lax.ppermute(block, AXES, pairs_of(move))]
    unnamed x12 -> x6, local copies, waits for them, and re-layouts: 5.39 us -> 0.02 us
    pallas_call x19 -> x21, Pallas kernels: 39.5 us -> 40.2 us  [call(): result = run(*args)]
  transfers between devices with their start and end apart: 25 -> 23, of which waited for: 7 -> 5; matrix products, arithmetic and copies ran while one was open for 3% -> 2% of each run, Pallas kernels for 31% -> 37%
where the time goes in v2:
time: 106 us
  starting transfers between devices  47.6 us (45%)
  Pallas kernels  40.2 us (38%)
  waiting for transfers between devices  14.4 us (14%)
  local copies, waits for them, and re-layouts  1.38 us (1%)
  other arithmetic  1.16 us (1%)
    ppermute x18, starting transfers between devices, send(): return lax.ppermute(block, AXES, pairs_of(move))  41.5 us
    pallas_call x21, Pallas kernels, call(): result = run(*args)  40.2 us
    ppermute x18, waiting for transfers between devices, send(): return lax.ppermute(block, AXES, pairs_of(move))  14.4 us
    ppermute x1, starting transfers between devices, swap_in_steps(): return lax.ppermute(block, 'rows', [(i, i ^ 3) for i in range(count)])  2.47 us
  transfers between devices with their start and end apart: 23, of which 5 were waited for; matrix products, arithmetic and copies ran while one was open for 2% of the time, Pallas kernels for 37%

profile of v2, /device:TPU:0, one launch (start us, length us, event | category | flops | bytes accessed | tf_op | source)
XLA Modules:
  0.0 105.6 jit_solution(10040305721801210409)
XLA Ops:
  2.6 3.5 %collective-permute-start.1 = (bf16[4,64,384]{2,1,0:T(8,128)(2,1)S(1)}, bf16[4,64,384]{2,1,0:T(8,128)(2,1)S(1)}, u32[]{:S(2)}, u32[]{:S(2)}) collective-permute-start(bf16[4,64,384]{2,1,0:T(8,128)(2,1)S(1)} %get-tuple-element.65), channel_id=1, source_target_pairs={{0,1},{1,0},{64,65},{65,64},{2,3},{3,2},{66,67},{67,66},{4,5},{5,4... | collective-permute-start | bytes 589832 | tf_op jit(solution)/shard_map/ppermute | solution.py:80
  8.9 8.9 %shard_map.67 = (bf16[32,64,384]{2,1,0:T(8,128)(2,1)S(1)}, bf16[3,40,64,384]{3,2,1,0:T(8,128)(2,1)S(1)}, bf16[3456,384]{1,0:T(8,128)(2,1)S(1)}) custom-call(bf16[32,64,384]{2,1,0:T(8,128)(2,1)S(1)} %bitcast.16, bf16[3456,384]{1,0:T(8,128)(2,1)} %far_ref.1), custom_call_target="tpu_custom_call" | custom-call | flops 4227858432 | bytes 14352384 | tf_op jit(solution)/shard_map/pallas_call | solution.py:41
  18.8 2.6 %shard_map.68 = (bf16[32,64,384]{2,1,0:T(8,128)(2,1)S(1)}, bf16[3,40,64,384]{3,2,1,0:T(8,128)(2,1)S(1)}) custom-call(bf16[4,64,384]{2,1,0:T(8,128)(2,1)S(1)} %collective-permute-done.distant_ref, bf16[4,64,384]{2,1,0:T(8,128)(2,1)S(1)} %collective-permute-done.1.chip_ref, ...), custom_call_target="tpu_custom_call", output_to_operand_aliasing={{0}: (3, {}), {1}: (4, {})} | custom-call | flops 1207959552 | bytes 17989632 | tf_op jit(solution)/shard_map/pallas_call | solution.py:41
  22.9 2.8 %shard_map.72.total_ref = f32[32,64,384]{2,1,0:T(8,128)S(1)} custom-call(bf16[32,64,384]{2,1,0:T(8,128)(2,1)S(1)} %bitcast.14, bf16[32,64,384]{2,1,0:T(8,128)(2,1)S(1)} %collective-permute-done.5.chip_ref, bf16[2304,768]{1,0:T(8,128)(2,1)S(1)} %get-tuple-element.40.w_ref), custom_call_target="tpu_custom_call" | custom-call | flops 2415919104 | bytes 9830400 | tf_op jit(solution)/shard_map/pallas_call | solution.py:41
  26.6 4.8 %shard_map.75.refs_0_ = f32[3456,384]{1,0:T(8,128)S(1)} custom-call(bf16[3,40,64,384]{3,2,1,0:T(8,128)(2,1)S(1)} %get-tuple-element.39.near_ref, bf16[20,64,384]{2,1,0:T(8,128)(2,1)S(1)} %shard_map.74.masked_ref), custom_call_target="tpu_custom_call" | custom-call | flops 3397386240 | bytes 12189696 | tf_op jit(solution)/shard_map/pallas_call | solution.py:41
  32.0 4.0 %shard_map.76 = (f32[3456,384]{1,0:T(8,128)S(1)}, bf16[4,2,216,384]{3,2,1,0:T(8,128)(2,1)S(1)}) custom-call(bf16[3,40,64,384]{3,2,1,0:T(8,128)(2,1)S(1)} %get-tuple-element.39.near_ref, bf16[12,64,384]{2,1,0:T(8,128)(2,1)S(1)} %shard_map.73.masked_ref, f32[3456,384]{1,0:T(8,128)S(1)} %shard_map.75.refs_0_), custom_call_target="tpu_custom_call", output_to_operand_aliasing={{0}: (2, {})} | custom-call | flops 2038431744 | bytes 18432000 | tf_op jit(solution)/shard_map/pallas_call | solution.py:41
  36.0 13.6 %collective-permute-start.8 = (bf16[4,2,216,384]{3,2,1,0:T(8,128)(2,1)S(1)}, bf16[4,2,216,384]{3,2,1,0:T(8,128)(2,1)S(1)}, u32[]{:S(2)}, u32[]{:S(2)}) collective-permute-start(bf16[4,2,216,384]{3,2,1,0:T(8,128)(2,1)S(1)} %get-tuple-element.42), channel_id=1, source_target_pairs={{0,1},{1,0},{64,65},{65,64},{2,3},{3,2},{66,67},{67,66},{4,5},{5,4... | collective-permute-start | bytes 3981320 | tf_op jit(solution)/shard_map/ppermute | solution.py:80
  49.6 2.8 %shard_map.80.begun_ref = f32[3456,384]{1,0:T(8,128)S(1)} custom-call(bf16[32,64,384]{2,1,0:T(8,128)(2,1)S(1)} %get-tuple-element.37.own_ref.hidden_ref, bf16[32,64,384]{2,1,0:T(8,128)(2,1)S(1)} %bitcast.15, bf16[32,64,384]{2,1,0:T(8,128)(2,1)S(1)} %collective-permute-done.5.chip_ref), custom_call_target="tpu_custom_call" | custom-call | flops 2415919104 | bytes 10027008 | tf_op jit(solution)/shard_map/pallas_call | solution.py:41
  55.4 2.5 %collective-permute-start.4 = (bf16[32,64,384]{2,1,0:T(8,128)(2,1)S(1)}, bf16[32,64,384]{2,1,0:T(8,128)(2,1)S(1)}, u32[]{:S(2)}, u32[]{:S(2)}) collective-permute-start(bf16[32,64,384]{2,1,0:T(8,128)(2,1)S(1)} %collective-permute-done.3), channel_id=1, source_target_pairs={{0,3},{1,2},{2,1},{3,0},{4,7},{5,6},{6,5},{7,4},{8,11},{9,10},{10,... | collective-permute-start | bytes 4718600 | tf_op jit(solution)/shard_map/ppermute | solution.py:487
  58.9 1.6 %collective-permute-start.9 = (bf16[2,2,216,384]{3,2,1,0:T(8,128)(2,1)S(1)}, bf16[2,2,216,384]{3,2,1,0:T(8,128)(2,1)S(1)}, u32[]{:S(2)}, u32[]{:S(2)}) collective-permute-start(bf16[2,2,216,384]{3,2,1,0:T(8,128)(2,1)S(1)} %get-tuple-element.44), channel_id=1, source_target_pairs={{0,16},{1,49},{64,80},{65,113},{2,18},{3,51},{66,82},{67,115},{4,2... | collective-permute-start | bytes 1990664 | tf_op jit(solution)/shard_map/ppermute | solution.py:80
  60.8 1.7 %collective-permute-start.15 = (bf16[2,2,216,384]{3,2,1,0:T(8,128)(2,1)S(1)}, bf16[2,2,216,384]{3,2,1,0:T(8,128)(2,1)S(1)}, u32[]{:S(2)}, u32[]{:S(2)}) collective-permute-start(bf16[2,2,216,384]{3,2,1,0:T(8,128)(2,1)S(1)} %get-tuple-element.53), channel_id=1, source_target_pairs={{0,4},{1,13},{64,68},{65,77},{2,6},{3,15},{66,70},{67,79},{4,0},{5... | collective-permute-start | bytes 1990664 | tf_op jit(solution)/shard_map/ppermute | solution.py:80
  62.4 7.2 %collective-permute-done.9.got_ref = bf16[2,2,216,384]{3,2,1,0:T(8,128)(2,1)S(1)} collective-permute-done((bf16[2,2,216,384]{3,2,1,0:T(8,128)(2,1)S(1)}, bf16[2,2,216,384]{3,2,1,0:T(8,128)(2,1)S(1)}, u32[]{:S(2)}, u32[]{:S(2)}) %collective-permute-start.9) | collective-permute-done | bytes 663584 | tf_op jit(solution)/shard_map/ppermute | solution.py:80
  69.7 2.9 %collective-permute-start.10 = (bf16[2,216,384]{2,1,0:T(8,128)(2,1)S(1)}, bf16[2,216,384]{2,1,0:T(8,128)(2,1)S(1)}, u32[]{:S(2)}, u32[]{:S(2)}) collective-permute-start(bf16[2,216,384]{2,1,0:T(8,128)(2,1)S(1)} %shard_map.78), channel_id=1, source_target_pairs={{0,48},{1,17},{64,112},{65,81},{2,50},{3,19},{66,114},{67,83},{4,5... | collective-permute-start | bytes 995336 | tf_op jit(solution)/shard_map/ppermute | solution.py:80
  72.7 2.4 %collective-permute-start.16 = (bf16[2,216,384]{2,1,0:T(8,128)(2,1)S(1)}, bf16[2,216,384]{2,1,0:T(8,128)(2,1)S(1)}, u32[]{:S(2)}, u32[]{:S(2)}) collective-permute-start(bf16[2,216,384]{2,1,0:T(8,128)(2,1)S(1)} %shard_map.84), channel_id=1, source_target_pairs={{0,12},{1,5},{64,76},{65,69},{2,14},{3,7},{66,78},{67,71},{4,8},{5... | collective-permute-start | bytes 995336 | tf_op jit(solution)/shard_map/ppermute | solution.py:80
  75.1 3.0 %collective-permute-done.10.last_ref = bf16[2,216,384]{2,1,0:T(8,128)(2,1)S(1)} collective-permute-done((bf16[2,216,384]{2,1,0:T(8,128)(2,1)S(1)}, bf16[2,216,384]{2,1,0:T(8,128)(2,1)S(1)}, u32[]{:S(2)}, u32[]{:S(2)}) %collective-permute-start.10) | collective-permute-done | bytes 331808 | tf_op jit(solution)/shard_map/ppermute | solution.py:80
  78.8 1.7 %collective-permute-start.11 = (bf16[112,384]{1,0:T(8,128)(2,1)S(1)}, bf16[112,384]{1,0:T(8,128)(2,1)S(1)}, u32[]{:S(2)}, u32[]{:S(2)}) collective-permute-start(bf16[112,384]{1,0:T(8,128)(2,1)S(1)} %get-tuple-element.47), channel_id=1, source_target_pairs={{0,4},{1,5},{64,68},{65,69},{2,6},{3,7},{66,70},{67,71},{4,8},{5,9... | collective-permute-start | bytes 258056 | tf_op jit(solution)/shard_map/ppermute | solution.py:80
  80.4 2.2 %collective-permute-start.12 = (bf16[112,384]{1,0:T(8,128)(2,1)S(1)}, bf16[112,384]{1,0:T(8,128)(2,1)S(1)}, u32[]{:S(2)}, u32[]{:S(2)}) collective-permute-start(bf16[112,384]{1,0:T(8,128)(2,1)S(1)} %get-tuple-element.48), channel_id=1, source_target_pairs={{0,8},{1,9},{64,72},{65,73},{2,10},{3,11},{66,74},{67,75},{4,12},{... | collective-permute-start | bytes 258056 | tf_op jit(solution)/shard_map/ppermute | solution.py:80
  82.7 1.7 %collective-permute-start.13 = (bf16[112,384]{1,0:T(8,128)(2,1)S(1)}, bf16[112,384]{1,0:T(8,128)(2,1)S(1)}, u32[]{:S(2)}, u32[]{:S(2)}) collective-permute-start(bf16[112,384]{1,0:T(8,128)(2,1)S(1)} %get-tuple-element.49), channel_id=1, source_target_pairs={{0,12},{1,13},{64,76},{65,77},{2,14},{3,15},{66,78},{67,79},{4,0},... | collective-permute-start | bytes 258056 | tf_op jit(solution)/shard_map/ppermute | solution.py:80
  85.3 4.0 %collective-permute-start.18 = (bf16[112,384]{1,0:T(8,128)(2,1)S(1)}, bf16[112,384]{1,0:T(8,128)(2,1)S(1)}, u32[]{:S(2)}, u32[]{:S(2)}) collective-permute-start(bf16[112,384]{1,0:T(8,128)(2,1)S(1)} %get-tuple-element.57), channel_id=1, source_target_pairs={{0,32},{1,33},{64,96},{65,97},{2,34},{3,35},{66,98},{67,99},{4,36}... | collective-permute-start | bytes 258056 | tf_op jit(solution)/shard_map/ppermute | solution.py:80
  89.5 2.8 %shard_map.70.total_ref = f32[32,64,384]{2,1,0:T(8,128)S(1)} custom-call(bf16[32,64,384]{2,1,0:T(8,128)(2,1)S(1)} %get-tuple-element.37.own_ref.hidden_ref, bf16[32,64,384]{2,1,0:T(8,128)(2,1)S(1)} %collective-permute-done.2.chip_ref, bf16[2304,768]{1,0:T(8,128)(2,1)S(1)} %get-tuple-element.38.w_ref), custom_call_target="tpu_custom_call" | custom-call | flops 2415919104 | bytes 9830400 | tf_op jit(solution)/shard_map/pallas_call | solution.py:41
  94.4 1.5 %collective-permute-start.20 = (bf16[216,96]{1,0:T(8,128)(2,1)S(1)}, bf16[216,96]{1,0:T(8,128)(2,1)S(1)}, u32[]{:S(2)}, u32[]{:S(2)}) collective-permute-start(bf16[216,96]{1,0:T(8,128)(2,1)S(1)} %get-tuple-element.60), channel_id=1, source_target_pairs={{0,2},{1,3},{64,66},{65,67},{2,0},{3,1},{66,64},{67,65},{4,6},{5,7... | collective-permute-start | bytes 124424 | tf_op jit(solution)/shard_map/ppermute | solution.py:80
  95.9 3.6 %collective-permute-start.21 = (bf16[216,96]{1,0:T(8,128)(2,1)S(1)}, bf16[216,96]{1,0:T(8,128)(2,1)S(1)}, u32[]{:S(2)}, u32[]{:S(2)}) collective-permute-start(bf16[216,96]{1,0:T(8,128)(2,1)S(1)} %get-tuple-element.61), channel_id=1, source_target_pairs={{0,64},{1,65},{64,0},{65,1},{2,66},{3,67},{66,2},{67,3},{4,68},{5,... | collective-permute-start | bytes 124424 | tf_op jit(solution)/shard_map/ppermute | solution.py:80
  99.5 2.7 %shard_map.71 = bf16[32,64,384]{2,1,0:T(8,128)(2,1)} custom-call(f32[32,64,384]{2,1,0:T(8,128)S(1)} %shard_map.70.total_ref, bf16[32,64,384]{2,1,0:T(8,128)(2,1)S(1)} %collective-permute-done.4.distant_ref, bf16[2304,768]{1,0:T(8,128)(2,1)S(1)} %get-tuple-element.38.w_ref), custom_call_target="tpu_custom_call" | custom-call | flops 1207959552 | bytes 9830400 | tf_op jit(solution)/shard_map/pallas_call | solution.py:41
  102.2 2.6 %collective-permute-done.22.r3 = bf16[216,96]{1,0:T(8,128)(2,1)S(1)} collective-permute-done((bf16[216,96]{1,0:T(8,128)(2,1)S(1)}, bf16[216,96]{1,0:T(8,128)(2,1)S(1)}, u32[]{:S(2)}, u32[]{:S(2)}) %collective-permute-start.22) | collective-permute-done | bytes 41504 | tf_op jit(solution)/shard_map/ppermute | solution.py:80
  (52 shorter events, 17.7 us)
Async XLA Ops:
  0.6 22.2 %collective-permute-start.5 = (bf16[32,64,384]{2,1,0:T(8,128)(2,1)}, bf16[32,64,384]{2,1,0:T(8,128)(2,1)S(1)}, u32[]{:S(2)}, u32[]{:S(2)}) collective-permute-start(bf16[32,64,384]{2,1,0:T(8,128)(2,1)} %bitcast.13), channel_id=1, source_target_pairs={{0,1},{1,0},{64,65},{65,64},{2,3},{3,2},{66,67},{67,66},{4,5},{5,4... | collective-permute-start | bytes 4718600 | tf_op jit(solution)/shard_map/ppermute | solution.py:80
  1.9 16.8 %collective-permute-start = (bf16[4,64,384]{2,1,0:T(8,128)(2,1)S(1)}, bf16[4,64,384]{2,1,0:T(8,128)(2,1)S(1)}, u32[]{:S(2)}, u32[]{:S(2)}) collective-permute-start(bf16[4,64,384]{2,1,0:T(8,128)(2,1)S(1)} %get-tuple-element.66), channel_id=1, source_target_pairs={{1,2},{3,4},{5,6},{7,8},{9,10},{11,12},{13,14},{2,1},{4,3},{6,5},{... | collective-permute-start | bytes 589832 | tf_op jit(solution)/shard_map/ppermute | solution.py:478
  2.6 16.1 %collective-permute-start.1 = (bf16[4,64,384]{2,1,0:T(8,128)(2,1)S(1)}, bf16[4,64,384]{2,1,0:T(8,128)(2,1)S(1)}, u32[]{:S(2)}, u32[]{:S(2)}) collective-permute-start(bf16[4,64,384]{2,1,0:T(8,128)(2,1)S(1)} %get-tuple-element.65), channel_id=1, source_target_pairs={{0,1},{1,0},{64,65},{65,64},{2,3},{3,2},{66,67},{67,66},{4,5},{5,4... | collective-permute-start | bytes 589832 | tf_op jit(solution)/shard_map/ppermute | solution.py:80
  7.4 18.3 %collective-permute-start.7 = (bf16[20,64,384]{2,1,0:T(8,128)(2,1)S(1)}, bf16[20,64,384]{2,1,0:T(8,128)(2,1)S(1)}, u32[]{:S(2)}, u32[]{:S(2)}) collective-permute-start(bf16[20,64,384]{2,1,0:T(8,128)(2,1)S(1)} %slice_bitcast_fusion), channel_id=1, source_target_pairs={{1,2},{3,4},{5,6},{7,8},{9,10},{11,12},{13,14},{2,1},{4,3},{6,5},{... | collective-permute-start | bytes 2949128 | tf_op jit(solution)/shard_map/ppermute | solution.py:478
  8.2 23.2 %collective-permute-start.6 = (bf16[12,64,384]{2,1,0:T(8,128)(2,1)S(1)}, bf16[12,64,384]{2,1,0:T(8,128)(2,1)S(1)}, u32[]{:S(2)}, u32[]{:S(2)}) collective-permute-start(bf16[12,64,384]{2,1,0:T(8,128)(2,1)S(1)} %slice_bitcast_fusion.1), channel_id=1, source_target_pairs={{1,2},{3,4},{5,6},{7,8},{9,10},{11,12},{13,14},{2,1},{4,3},{6,5},{... | collective-permute-start | bytes 1769480 | tf_op jit(solution)/shard_map/ppermute | solution.py:478
  8.9 8.9 %copy-start.1 = (bf16[3456,384]{1,0:T(8,128)(2,1)S(1)}, bf16[3456,384]{1,0:T(8,128)(2,1)}, u32[]{:S(2)}) copy-start(bf16[3456,384]{1,0:T(8,128)(2,1)} %w_ref.1) | copy-start | bytes 7962628
  21.4 34.1 %collective-permute-start.3 = (bf16[32,64,384]{2,1,0:T(8,128)(2,1)S(1)}, bf16[32,64,384]{2,1,0:T(8,128)(2,1)S(1)}, u32[]{:S(2)}, u32[]{:S(2)}) collective-permute-start(bf16[32,64,384]{2,1,0:T(8,128)(2,1)S(1)} %get-tuple-element.37.own_ref.hidden_ref), channel_id=1, source_target_pairs={{1,1},{2,2},{5,5},{6,6},{9,9},{10,10},{13,13},{14,14},{3,7},{4,0},... | collective-permute-start | bytes 4718600 | tf_op jit(solution)/shard_map/ppermute | solution.py:486
  36.0 21.9 %collective-permute-start.8 = (bf16[4,2,216,384]{3,2,1,0:T(8,128)(2,1)S(1)}, bf16[4,2,216,384]{3,2,1,0:T(8,128)(2,1)S(1)}, u32[]{:S(2)}, u32[]{:S(2)}) collective-permute-start(bf16[4,2,216,384]{3,2,1,0:T(8,128)(2,1)S(1)} %get-tuple-element.42), channel_id=1, source_target_pairs={{0,1},{1,0},{64,65},{65,64},{2,3},{3,2},{66,67},{67,66},{4,5},{5,4... | collective-permute-start | bytes 3981320 | tf_op jit(solution)/shard_map/ppermute | solution.py:80
  54.8 5.7 %collective-permute-start.14 = (bf16[4,2,216,384]{3,2,1,0:T(8,128)(2,1)S(1)}, bf16[4,2,216,384]{3,2,1,0:T(8,128)(2,1)S(1)}, u32[]{:S(2)}, u32[]{:S(2)}) collective-permute-start(bf16[4,2,216,384]{3,2,1,0:T(8,128)(2,1)S(1)} %get-tuple-element.51), channel_id=1, source_target_pairs={{0,1},{1,0},{64,65},{65,64},{2,3},{3,2},{66,67},{67,66},{4,5},{5,4... | collective-permute-start | bytes 3981320 | tf_op jit(solution)/shard_map/ppermute | solution.py:80
  54.9 30.0 %collective-permute-start.2 = (bf16[32,64,384]{2,1,0:T(8,128)(2,1)S(1)}, bf16[32,64,384]{2,1,0:T(8,128)(2,1)S(1)}, u32[]{:S(2)}, u32[]{:S(2)}) collective-permute-start(bf16[32,64,384]{2,1,0:T(8,128)(2,1)S(1)} %get-tuple-element.37.own_ref.hidden_ref), channel_id=1, source_target_pairs={{0,1},{1,0},{64,65},{65,64},{2,3},{3,2},{66,67},{67,66},{4,5},{5,4... | collective-permute-start | bytes 4718600 | tf_op jit(solution)/shard_map/ppermute | solution.py:80
  55.4 44.1 %collective-permute-start.4 = (bf16[32,64,384]{2,1,0:T(8,128)(2,1)S(1)}, bf16[32,64,384]{2,1,0:T(8,128)(2,1)S(1)}, u32[]{:S(2)}, u32[]{:S(2)}) collective-permute-start(bf16[32,64,384]{2,1,0:T(8,128)(2,1)S(1)} %collective-permute-done.3), channel_id=1, source_target_pairs={{0,3},{1,2},{2,1},{3,0},{4,7},{5,6},{6,5},{7,4},{8,11},{9,10},{10,... | collective-permute-start | bytes 4718600 | tf_op jit(solution)/shard_map/ppermute | solution.py:487
  58.9 10.8 %collective-permute-start.9 = (bf16[2,2,216,384]{3,2,1,0:T(8,128)(2,1)S(1)}, bf16[2,2,216,384]{3,2,1,0:T(8,128)(2,1)S(1)}, u32[]{:S(2)}, u32[]{:S(2)}) collective-permute-start(bf16[2,2,216,384]{3,2,1,0:T(8,128)(2,1)S(1)} %get-tuple-element.44), channel_id=1, source_target_pairs={{0,16},{1,49},{64,80},{65,113},{2,18},{3,51},{66,82},{67,115},{4,2... | collective-permute-start | bytes 1990664 | tf_op jit(solution)/shard_map/ppermute | solution.py:80
  60.8 11.8 %collective-permute-start.15 = (bf16[2,2,216,384]{3,2,1,0:T(8,128)(2,1)S(1)}, bf16[2,2,216,384]{3,2,1,0:T(8,128)(2,1)S(1)}, u32[]{:S(2)}, u32[]{:S(2)}) collective-permute-start(bf16[2,2,216,384]{3,2,1,0:T(8,128)(2,1)S(1)} %get-tuple-element.53), channel_id=1, source_target_pairs={{0,4},{1,13},{64,68},{65,77},{2,6},{3,15},{66,70},{67,79},{4,0},{5... | collective-permute-start | bytes 1990664 | tf_op jit(solution)/shard_map/ppermute | solution.py:80
  69.7 8.4 %collective-permute-start.10 = (bf16[2,216,384]{2,1,0:T(8,128)(2,1)S(1)}, bf16[2,216,384]{2,1,0:T(8,128)(2,1)S(1)}, u32[]{:S(2)}, u32[]{:S(2)}) collective-permute-start(bf16[2,216,384]{2,1,0:T(8,128)(2,1)S(1)} %shard_map.78), channel_id=1, source_target_pairs={{0,48},{1,17},{64,112},{65,81},{2,50},{3,19},{66,114},{67,83},{4,5... | collective-permute-start | bytes 995336 | tf_op jit(solution)/shard_map/ppermute | solution.py:80
  72.7 10.0 %collective-permute-start.16 = (bf16[2,216,384]{2,1,0:T(8,128)(2,1)S(1)}, bf16[2,216,384]{2,1,0:T(8,128)(2,1)S(1)}, u32[]{:S(2)}, u32[]{:S(2)}) collective-permute-start(bf16[2,216,384]{2,1,0:T(8,128)(2,1)S(1)} %shard_map.84), channel_id=1, source_target_pairs={{0,12},{1,5},{64,76},{65,69},{2,14},{3,7},{66,78},{67,71},{4,8},{5... | collective-permute-start | bytes 995336 | tf_op jit(solution)/shard_map/ppermute | solution.py:80
  78.8 6.6 %collective-permute-start.11 = (bf16[112,384]{1,0:T(8,128)(2,1)S(1)}, bf16[112,384]{1,0:T(8,128)(2,1)S(1)}, u32[]{:S(2)}, u32[]{:S(2)}) collective-permute-start(bf16[112,384]{1,0:T(8,128)(2,1)S(1)} %get-tuple-element.47), channel_id=1, source_target_pairs={{0,4},{1,5},{64,68},{65,69},{2,6},{3,7},{66,70},{67,71},{4,8},{5,9... | collective-permute-start | bytes 258056 | tf_op jit(solution)/shard_map/ppermute | solution.py:80
  80.4 8.9 %collective-permute-start.12 = (bf16[112,384]{1,0:T(8,128)(2,1)S(1)}, bf16[112,384]{1,0:T(8,128)(2,1)S(1)}, u32[]{:S(2)}, u32[]{:S(2)}) collective-permute-start(bf16[112,384]{1,0:T(8,128)(2,1)S(1)} %get-tuple-element.48), channel_id=1, source_target_pairs={{0,8},{1,9},{64,72},{65,73},{2,10},{3,11},{66,74},{67,75},{4,12},{... | collective-permute-start | bytes 258056 | tf_op jit(solution)/shard_map/ppermute | solution.py:80
  82.7 9.6 %collective-permute-start.13 = (bf16[112,384]{1,0:T(8,128)(2,1)S(1)}, bf16[112,384]{1,0:T(8,128)(2,1)S(1)}, u32[]{:S(2)}, u32[]{:S(2)}) collective-permute-start(bf16[112,384]{1,0:T(8,128)(2,1)S(1)} %get-tuple-element.49), channel_id=1, source_target_pairs={{0,12},{1,13},{64,76},{65,77},{2,14},{3,15},{66,78},{67,79},{4,0},... | collective-permute-start | bytes 258056 | tf_op jit(solution)/shard_map/ppermute | solution.py:80
  85.0 7.3 %collective-permute-start.17 = (bf16[112,384]{1,0:T(8,128)(2,1)S(1)}, bf16[112,384]{1,0:T(8,128)(2,1)S(1)}, u32[]{:S(2)}, u32[]{:S(2)}) collective-permute-start(bf16[112,384]{1,0:T(8,128)(2,1)S(1)} %get-tuple-element.56), channel_id=1, source_target_pairs={{0,16},{1,17},{64,80},{65,81},{2,18},{3,19},{66,82},{67,83},{4,20}... | collective-permute-start | bytes 258056 | tf_op jit(solution)/shard_map/ppermute | solution.py:80
  85.3 7.3 %collective-permute-start.18 = (bf16[112,384]{1,0:T(8,128)(2,1)S(1)}, bf16[112,384]{1,0:T(8,128)(2,1)S(1)}, u32[]{:S(2)}, u32[]{:S(2)}) collective-permute-start(bf16[112,384]{1,0:T(8,128)(2,1)S(1)} %get-tuple-element.57), channel_id=1, source_target_pairs={{0,32},{1,33},{64,96},{65,97},{2,34},{3,35},{66,98},{67,99},{4,36}... | collective-permute-start | bytes 258056 | tf_op jit(solution)/shard_map/ppermute | solution.py:80
  89.3 4.5 %collective-permute-start.19 = (bf16[112,384]{1,0:T(8,128)(2,1)S(1)}, bf16[112,384]{1,0:T(8,128)(2,1)S(1)}, u32[]{:S(2)}, u32[]{:S(2)}) collective-permute-start(bf16[112,384]{1,0:T(8,128)(2,1)S(1)} %get-tuple-element.58), channel_id=1, source_target_pairs={{0,48},{1,49},{64,112},{65,113},{2,50},{3,51},{66,114},{67,115},{4... | collective-permute-start | bytes 258056 | tf_op jit(solution)/shard_map/ppermute | solution.py:80
  94.4 7.9 %collective-permute-start.20 = (bf16[216,96]{1,0:T(8,128)(2,1)S(1)}, bf16[216,96]{1,0:T(8,128)(2,1)S(1)}, u32[]{:S(2)}, u32[]{:S(2)}) collective-permute-start(bf16[216,96]{1,0:T(8,128)(2,1)S(1)} %get-tuple-element.60), channel_id=1, source_target_pairs={{0,2},{1,3},{64,66},{65,67},{2,0},{3,1},{66,64},{67,65},{4,6},{5,7... | collective-permute-start | bytes 124424 | tf_op jit(solution)/shard_map/ppermute | solution.py:80
  95.9 6.3 %collective-permute-start.21 = (bf16[216,96]{1,0:T(8,128)(2,1)S(1)}, bf16[216,96]{1,0:T(8,128)(2,1)S(1)}, u32[]{:S(2)}, u32[]{:S(2)}) collective-permute-start(bf16[216,96]{1,0:T(8,128)(2,1)S(1)} %get-tuple-element.61), channel_id=1, source_target_pairs={{0,64},{1,65},{64,0},{65,1},{2,66},{3,67},{66,2},{67,3},{4,68},{5,... | collective-permute-start | bytes 124424 | tf_op jit(solution)/shard_map/ppermute | solution.py:80
  99.5 5.4 %collective-permute-start.22 = (bf16[216,96]{1,0:T(8,128)(2,1)S(1)}, bf16[216,96]{1,0:T(8,128)(2,1)S(1)}, u32[]{:S(2)}, u32[]{:S(2)}) collective-permute-start(bf16[216,96]{1,0:T(8,128)(2,1)S(1)} %get-tuple-element.62), channel_id=1, source_target_pairs={{0,66},{1,67},{64,2},{65,3},{2,64},{3,65},{66,0},{67,1},{4,70},{5,... | collective-permute-start | bytes 124424 | tf_op jit(solution)/shard_map/ppermute | solution.py:80
  (2 other events, 13.8 us)

commit v3 on v2

--- a/solution.py
+++ b/solution.py
@@ -20,7 +20,7 @@
 SLIM = 48
 TALL = 112
 WHOLE = pl.BlockSpec(memory_space=pltpu.VMEM)
-PARTS = ((0, 20), (20, 12))
+PARTS = ((0, 16), (16, 8), (24, 8))
 AXES = ("dp", "rows")
 
 
@@ -78,6 +78,20 @@
 
 def send(block, move):
     return lax.ppermute(block, AXES, pairs_of(move))
+
+
+def stage_kernel(picture_ref, upstream_ref, distant_ref, chip_ref, part_ref, sems):
+    core = place()[4]
+    edge = ROWS - 4
+    copies = (
+        pltpu.make_async_copy(picture_ref.at[pl.ds(edge * core, 4)], distant_ref, sems.at[0]),
+        pltpu.make_async_copy(picture_ref.at[pl.ds(edge * (1 - core), 4)], chip_ref, sems.at[1]),
+        pltpu.make_async_copy(upstream_ref.at[pl.ds(0, PARTS[0][1])], part_ref, sems.at[2]),
+    )
+    for copy in copies:
+        copy.start()
+    for copy in copies:
+        copy.wait()
 
 
 def weight_kernel(w_ref, forward_ref, backward_ref):
@@ -492,12 +506,19 @@
     upstream = cotangent[0]
     factor = 1.0 / math.sqrt(lax.axis_size("dp") * ROWS * lax.axis_size("rows") * COLS)
     work = 2 * ROWS * COLS * CH * CH
-    first_core = lax.rem(lax.axis_index("rows"), 2) == 0
-    head, tail = picture[:4], picture[-4:]
-    edge_distant = swap_distant(jnp.where(first_core, head, tail))
-    edge_chip = swap_chip(jnp.where(first_core, tail, head))
     part_kinds = [shape_of((count, COLS, CH), BF16) for _, count in PARTS]
-    c_parts = [swap_distant(upstream[first : first + count]) for first, count in PARTS]
+    edge_kind = shape_of((4, COLS, CH), BF16)
+    edge_distant, edge_chip, first_part = call(
+        stage_kernel,
+        [edge_kind, edge_kind, part_kinds[0]],
+        [pltpu.with_memory_space_constraint(a, pltpu.HBM) for a in (picture, upstream)],
+        scratch=[pltpu.SemaphoreType.DMA((3,))],
+        where=[pl.BlockSpec(memory_space=pltpu.HBM)] * 2,
+    )
+    edge_distant = swap_distant(edge_distant)
+    edge_chip = swap_chip(edge_chip)
+    c_parts = [first_part] + [upstream[first : first + count] for first, count in PARTS[1:]]
+    c_parts = [swap_distant(part) for part in c_parts]
     c_chip = swap_chip(upstream)
     kind = shape_of((6 * CH, 2 * CH), BF16)
     forward_w, backward_w = call(weight_kernel, [kind, kind], (weight_two,))

time: 106 us -> 108 us (1.019)
  Pallas kernels: 40.2 us -> 42.5 us
  starting transfers between devices: 47.6 us -> 49 us
  local copies, waits for them, and re-layouts: 1.38 us -> 0.1 us
  other arithmetic: 1.16 us -> 0 us
    pallas_call x21 -> x25, Pallas kernels: 40.2 us -> 42.5 us  [call(): result = run(*args)]
    slice x2 -> x1, local copies, waits for them, and re-layouts: 1.36 us -> 0.08 us  [on_device(): upstream[first:first + count]]
    select_n x1 -> x0, other arithmetic: 1.16 us -> none  [on_device(): edge_chip = swap_chip(jnp.where(first_core, tail, head))]
    ppermute x3 -> x4, starting transfers between devices: 2.1 us -> 2.88 us  [swap_distant(): return lax.ppermute(block, 'rows', pairs + [(j, i) for i, j in pairs])]
  transfers between devices with their start and end apart: 23 -> 24, of which waited for: 5 -> 5; matrix products, arithmetic and copies ran while one was open for 2% -> 0% of each run, Pallas kernels for 37% -> 39%
where the time goes in v3:
time: 108 us
  starting transfers between devices  49 us (45%)
  Pallas kernels  42.5 us (39%)
  waiting for transfers between devices  14.9 us (14%)
    pallas_call x25, Pallas kernels, call(): result = run(*args)  42.5 us
    ppermute x18, starting transfers between devices, send(): return lax.ppermute(block, AXES, pairs_of(move))  42.2 us
    ppermute x18, waiting for transfers between devices, send(): return lax.ppermute(block, AXES, pairs_of(move))  14.9 us
    ppermute x4, starting transfers between devices, swap_distant(): return lax.ppermute(block, 'rows', pairs + [(j, i) for i, j in pairs])  2.88 us
    ppermute x1, starting transfers between devices, swap_in_steps(): return lax.ppermute(block, 'rows', [(i, i ^ 3) for i in range(count)])  2.46 us
  transfers between devices with their start and end apart: 24, of which 5 were waited for; matrix products, arithmetic and copies ran while one was open for 0% of the time, Pallas kernels for 39%

profile of v3, /device:TPU:0, one launch (start us, length us, event | category | flops | bytes accessed | tf_op | source)
XLA Modules:
  0.0 107.5 jit_solution(6796125647304881410)
XLA Ops:
  2.9 3.5 %collective-permute-start.1 = (bf16[4,64,384]{2,1,0:T(8,128)(2,1)S(1)}, bf16[4,64,384]{2,1,0:T(8,128)(2,1)S(1)}, u32[]{:S(2)}, u32[]{:S(2)}) collective-permute-start(bf16[4,64,384]{2,1,0:T(8,128)(2,1)S(1)} %get-tuple-element.38), channel_id=1, source_target_pairs={{0,1},{1,0},{64,65},{65,64},{2,3},{3,2},{66,67},{67,66},{4,5},{5,4... | collective-permute-start | bytes 589832 | tf_op jit(solution)/shard_map/ppermute | solution.py:80
  8.1 8.9 %shard_map.68 = (bf16[32,64,384]{2,1,0:T(8,128)(2,1)S(1)}, bf16[3,40,64,384]{3,2,1,0:T(8,128)(2,1)S(1)}, bf16[3456,384]{1,0:T(8,128)(2,1)S(1)}) custom-call(bf16[32,64,384]{2,1,0:T(8,128)(2,1)S(1)} %bitcast.14, bf16[3456,384]{1,0:T(8,128)(2,1)} %far_ref.1), custom_call_target="tpu_custom_call" | custom-call | flops 4227858432 | bytes 14352384 | tf_op jit(solution)/shard_map/pallas_call | solution.py:41
  18.6 2.7 %shard_map.69 = (bf16[32,64,384]{2,1,0:T(8,128)(2,1)S(1)}, bf16[3,40,64,384]{3,2,1,0:T(8,128)(2,1)S(1)}) custom-call(bf16[4,64,384]{2,1,0:T(8,128)(2,1)S(1)} %collective-permute-done.distant_ref, bf16[4,64,384]{2,1,0:T(8,128)(2,1)S(1)} %collective-permute-done.1.chip_ref, ...), custom_call_target="tpu_custom_call", output_to_operand_aliasing={{0}: (3, {}), {1}: (4, {})} | custom-call | flops 1207959552 | bytes 17989632 | tf_op jit(solution)/shard_map/pallas_call | solution.py:41
  22.8 2.8 %shard_map.73.total_ref = f32[32,64,384]{2,1,0:T(8,128)S(1)} custom-call(bf16[32,64,384]{2,1,0:T(8,128)(2,1)S(1)} %bitcast.11, bf16[32,64,384]{2,1,0:T(8,128)(2,1)S(1)} %collective-permute-done.5.chip_ref, bf16[2304,768]{1,0:T(8,128)(2,1)S(1)} %get-tuple-element.45.w_ref), custom_call_target="tpu_custom_call" | custom-call | flops 2415919104 | bytes 9830400 | tf_op jit(solution)/shard_map/pallas_call | solution.py:41
  27.0 3.9 %shard_map.77.refs_0_ = f32[3456,384]{1,0:T(8,128)S(1)} custom-call(bf16[3,40,64,384]{3,2,1,0:T(8,128)(2,1)S(1)} %get-tuple-element.44.near_ref, bf16[16,64,384]{2,1,0:T(8,128)(2,1)S(1)} %shard_map.76.masked_ref), custom_call_target="tpu_custom_call" | custom-call | flops 2717908992 | bytes 11993088 | tf_op jit(solution)/shard_map/pallas_call | solution.py:41
  31.4 2.1 %shard_map.78.refs_0_ = f32[3456,384]{1,0:T(8,128)S(1)} custom-call(bf16[3,40,64,384]{3,2,1,0:T(8,128)(2,1)S(1)} %get-tuple-element.44.near_ref, bf16[8,64,384]{2,1,0:T(8,128)(2,1)S(1)} %shard_map.75.masked_ref, f32[3456,384]{1,0:T(8,128)S(1)} %shard_map.77.refs_0_), custom_call_target="tpu_custom_call", output_to_operand_aliasing={{}: (2, {})} | custom-call | flops 1358954496 | bytes 16908288 | tf_op jit(solution)/shard_map/pallas_call | solution.py:41
  33.5 3.1 %shard_map.79 = (f32[3456,384]{1,0:T(8,128)S(1)}, bf16[4,2,216,384]{3,2,1,0:T(8,128)(2,1)S(1)}) custom-call(bf16[3,40,64,384]{3,2,1,0:T(8,128)(2,1)S(1)} %get-tuple-element.44.near_ref, bf16[8,64,384]{2,1,0:T(8,128)(2,1)S(1)} %shard_map.74.masked_ref, f32[3456,384]{1,0:T(8,128)S(1)} %shard_map.78.refs_0_), custom_call_target="tpu_custom_call", output_to_operand_aliasing={{0}: (2, {})} | custom-call | flops 1358954496 | bytes 18235392 | tf_op jit(solution)/shard_map/pallas_call | solution.py:41
  36.6 15.2 %collective-permute-start.9 = (bf16[4,2,216,384]{3,2,1,0:T(8,128)(2,1)S(1)}, bf16[4,2,216,384]{3,2,1,0:T(8,128)(2,1)S(1)}, u32[]{:S(2)}, u32[]{:S(2)}) collective-permute-start(bf16[4,2,216,384]{3,2,1,0:T(8,128)(2,1)S(1)} %get-tuple-element.48), channel_id=1, source_target_pairs={{0,1},{1,0},{64,65},{65,64},{2,3},{3,2},{66,67},{67,66},{4,5},{5,4... | collective-permute-start | bytes 3981320 | tf_op jit(solution)/shard_map/ppermute | solution.py:80
  51.9 2.9 %shard_map.83.begun_ref = f32[3456,384]{1,0:T(8,128)S(1)} custom-call(bf16[32,64,384]{2,1,0:T(8,128)(2,1)S(1)} %get-tuple-element.42.own_ref.hidden_ref, bf16[32,64,384]{2,1,0:T(8,128)(2,1)S(1)} %bitcast.12, bf16[32,64,384]{2,1,0:T(8,128)(2,1)S(1)} %collective-permute-done.5.chip_ref), custom_call_target="tpu_custom_call" | custom-call | flops 2415919104 | bytes 10027008 | tf_op jit(solution)/shard_map/pallas_call | solution.py:41
  57.8 2.5 %collective-permute-start.4 = (bf16[32,64,384]{2,1,0:T(8,128)(2,1)S(1)}, bf16[32,64,384]{2,1,0:T(8,128)(2,1)S(1)}, u32[]{:S(2)}, u32[]{:S(2)}) collective-permute-start(bf16[32,64,384]{2,1,0:T(8,128)(2,1)S(1)} %collective-permute-done.3), channel_id=1, source_target_pairs={{0,3},{1,2},{2,1},{3,0},{4,7},{5,6},{6,5},{7,4},{8,11},{9,10},{10,... | collective-permute-start | bytes 4718600 | tf_op jit(solution)/shard_map/ppermute | solution.py:501
  61.2 1.6 %collective-permute-start.10 = (bf16[2,2,216,384]{3,2,1,0:T(8,128)(2,1)S(1)}, bf16[2,2,216,384]{3,2,1,0:T(8,128)(2,1)S(1)}, u32[]{:S(2)}, u32[]{:S(2)}) collective-permute-start(bf16[2,2,216,384]{3,2,1,0:T(8,128)(2,1)S(1)} %get-tuple-element.50), channel_id=1, source_target_pairs={{0,16},{1,49},{64,80},{65,113},{2,18},{3,51},{66,82},{67,115},{4,2... | collective-permute-start | bytes 1990664 | tf_op jit(solution)/shard_map/ppermute | solution.py:80
  63.1 1.6 %collective-permute-start.16 = (bf16[2,2,216,384]{3,2,1,0:T(8,128)(2,1)S(1)}, bf16[2,2,216,384]{3,2,1,0:T(8,128)(2,1)S(1)}, u32[]{:S(2)}, u32[]{:S(2)}) collective-permute-start(bf16[2,2,216,384]{3,2,1,0:T(8,128)(2,1)S(1)} %get-tuple-element.59), channel_id=1, source_target_pairs={{0,4},{1,13},{64,68},{65,77},{2,6},{3,15},{66,70},{67,79},{4,0},{5... | collective-permute-start | bytes 1990664 | tf_op jit(solution)/shard_map/ppermute | solution.py:80
  64.8 7.2 %collective-permute-done.10.got_ref = bf16[2,2,216,384]{3,2,1,0:T(8,128)(2,1)S(1)} collective-permute-done((bf16[2,2,216,384]{3,2,1,0:T(8,128)(2,1)S(1)}, bf16[2,2,216,384]{3,2,1,0:T(8,128)(2,1)S(1)}, u32[]{:S(2)}, u32[]{:S(2)}) %collective-permute-start.10) | collective-permute-done | bytes 663584 | tf_op jit(solution)/shard_map/ppermute | solution.py:80
  72.1 2.9 %collective-permute-start.11 = (bf16[2,216,384]{2,1,0:T(8,128)(2,1)S(1)}, bf16[2,216,384]{2,1,0:T(8,128)(2,1)S(1)}, u32[]{:S(2)}, u32[]{:S(2)}) collective-permute-start(bf16[2,216,384]{2,1,0:T(8,128)(2,1)S(1)} %shard_map.81), channel_id=1, source_target_pairs={{0,48},{1,17},{64,112},{65,81},{2,50},{3,19},{66,114},{67,83},{4,5... | collective-permute-start | bytes 995336 | tf_op jit(solution)/shard_map/ppermute | solution.py:80
  75.0 1.6 %collective-permute-start.17 = (bf16[2,216,384]{2,1,0:T(8,128)(2,1)S(1)}, bf16[2,216,384]{2,1,0:T(8,128)(2,1)S(1)}, u32[]{:S(2)}, u32[]{:S(2)}) collective-permute-start(bf16[2,216,384]{2,1,0:T(8,128)(2,1)S(1)} %shard_map.88), channel_id=1, source_target_pairs={{0,12},{1,5},{64,76},{65,69},{2,14},{3,7},{66,78},{67,71},{4,8},{5... | collective-permute-start | bytes 995336 | tf_op jit(solution)/shard_map/ppermute | solution.py:80
  76.6 3.9 %collective-permute-done.11.last_ref = bf16[2,216,384]{2,1,0:T(8,128)(2,1)S(1)} collective-permute-done((bf16[2,216,384]{2,1,0:T(8,128)(2,1)S(1)}, bf16[2,216,384]{2,1,0:T(8,128)(2,1)S(1)}, u32[]{:S(2)}, u32[]{:S(2)}) %collective-permute-start.11) | collective-permute-done | bytes 331808 | tf_op jit(solution)/shard_map/ppermute | solution.py:80
  81.1 1.7 %collective-permute-start.12 = (bf16[112,384]{1,0:T(8,128)(2,1)S(1)}, bf16[112,384]{1,0:T(8,128)(2,1)S(1)}, u32[]{:S(2)}, u32[]{:S(2)}) collective-permute-start(bf16[112,384]{1,0:T(8,128)(2,1)S(1)} %get-tuple-element.53), channel_id=1, source_target_pairs={{0,4},{1,5},{64,68},{65,69},{2,6},{3,7},{66,70},{67,71},{4,8},{5,9... | collective-permute-start | bytes 258056 | tf_op jit(solution)/shard_map/ppermute | solution.py:80
  82.7 1.7 %collective-permute-start.13 = (bf16[112,384]{1,0:T(8,128)(2,1)S(1)}, bf16[112,384]{1,0:T(8,128)(2,1)S(1)}, u32[]{:S(2)}, u32[]{:S(2)}) collective-permute-start(bf16[112,384]{1,0:T(8,128)(2,1)S(1)} %get-tuple-element.54), channel_id=1, source_target_pairs={{0,8},{1,9},{64,72},{65,73},{2,10},{3,11},{66,74},{67,75},{4,12},{... | collective-permute-start | bytes 258056 | tf_op jit(solution)/shard_map/ppermute | solution.py:80
  84.4 2.5 %collective-permute-start.14 = (bf16[112,384]{1,0:T(8,128)(2,1)S(1)}, bf16[112,384]{1,0:T(8,128)(2,1)S(1)}, u32[]{:S(2)}, u32[]{:S(2)}) collective-permute-start(bf16[112,384]{1,0:T(8,128)(2,1)S(1)} %get-tuple-element.55), channel_id=1, source_target_pairs={{0,12},{1,13},{64,76},{65,77},{2,14},{3,15},{66,78},{67,79},{4,0},... | collective-permute-start | bytes 258056 | tf_op jit(solution)/shard_map/ppermute | solution.py:80
  87.9 4.0 %collective-permute-start.19 = (bf16[112,384]{1,0:T(8,128)(2,1)S(1)}, bf16[112,384]{1,0:T(8,128)(2,1)S(1)}, u32[]{:S(2)}, u32[]{:S(2)}) collective-permute-start(bf16[112,384]{1,0:T(8,128)(2,1)S(1)} %get-tuple-element.63), channel_id=1, source_target_pairs={{0,32},{1,33},{64,96},{65,97},{2,34},{3,35},{66,98},{67,99},{4,36}... | collective-permute-start | bytes 258056 | tf_op jit(solution)/shard_map/ppermute | solution.py:80
  92.1 2.8 %shard_map.71.total_ref = f32[32,64,384]{2,1,0:T(8,128)S(1)} custom-call(bf16[32,64,384]{2,1,0:T(8,128)(2,1)S(1)} %get-tuple-element.42.own_ref.hidden_ref, bf16[32,64,384]{2,1,0:T(8,128)(2,1)S(1)} %collective-permute-done.2.chip_ref, bf16[2304,768]{1,0:T(8,128)(2,1)S(1)} %get-tuple-element.43.w_ref), custom_call_target="tpu_custom_call" | custom-call | flops 2415919104 | bytes 9830400 | tf_op jit(solution)/shard_map/pallas_call | solution.py:41
  97.5 3.9 %collective-permute-start.22 = (bf16[216,96]{1,0:T(8,128)(2,1)S(1)}, bf16[216,96]{1,0:T(8,128)(2,1)S(1)}, u32[]{:S(2)}, u32[]{:S(2)}) collective-permute-start(bf16[216,96]{1,0:T(8,128)(2,1)S(1)} %get-tuple-element.67), channel_id=1, source_target_pairs={{0,64},{1,65},{64,0},{65,1},{2,66},{3,67},{66,2},{67,3},{4,68},{5,... | collective-permute-start | bytes 124424 | tf_op jit(solution)/shard_map/ppermute | solution.py:80
  101.7 2.7 %shard_map.72 = bf16[32,64,384]{2,1,0:T(8,128)(2,1)} custom-call(f32[32,64,384]{2,1,0:T(8,128)S(1)} %shard_map.71.total_ref, bf16[32,64,384]{2,1,0:T(8,128)(2,1)S(1)} %collective-permute-done.4.distant_ref, bf16[2304,768]{1,0:T(8,128)(2,1)S(1)} %get-tuple-element.43.w_ref), custom_call_target="tpu_custom_call" | custom-call | flops 1207959552 | bytes 9830400 | tf_op jit(solution)/shard_map/pallas_call | solution.py:41
  104.5 2.3 %collective-permute-done.23.r3 = bf16[216,96]{1,0:T(8,128)(2,1)S(1)} collective-permute-done((bf16[216,96]{1,0:T(8,128)(2,1)S(1)}, bf16[216,96]{1,0:T(8,128)(2,1)S(1)}, u32[]{:S(2)}, u32[]{:S(2)}) %collective-permute-start.23) | collective-permute-done | bytes 41504 | tf_op jit(solution)/shard_map/ppermute | solution.py:80
  (56 shorter events, 18.7 us)
Async XLA Ops:
  0.6 22.1 %collective-permute-start.5 = (bf16[32,64,384]{2,1,0:T(8,128)(2,1)}, bf16[32,64,384]{2,1,0:T(8,128)(2,1)S(1)}, u32[]{:S(2)}, u32[]{:S(2)}) collective-permute-start(bf16[32,64,384]{2,1,0:T(8,128)(2,1)} %bitcast.9), channel_id=1, source_target_pairs={{0,1},{1,0},{64,65},{65,64},{2,3},{3,2},{66,67},{67,66},{4,5},{5,4... | collective-permute-start | bytes 4718600 | tf_op jit(solution)/shard_map/ppermute | solution.py:80
  2.3 15.6 %collective-permute-start = (bf16[4,64,384]{2,1,0:T(8,128)(2,1)S(1)}, bf16[4,64,384]{2,1,0:T(8,128)(2,1)S(1)}, u32[]{:S(2)}, u32[]{:S(2)}) collective-permute-start(bf16[4,64,384]{2,1,0:T(8,128)(2,1)S(1)} %get-tuple-element.37), channel_id=1, source_target_pairs={{1,2},{3,4},{5,6},{7,8},{9,10},{11,12},{13,14},{2,1},{4,3},{6,5},{... | collective-permute-start | bytes 589832 | tf_op jit(solution)/shard_map/ppermute | solution.py:492
  2.9 15.7 %collective-permute-start.1 = (bf16[4,64,384]{2,1,0:T(8,128)(2,1)S(1)}, bf16[4,64,384]{2,1,0:T(8,128)(2,1)S(1)}, u32[]{:S(2)}, u32[]{:S(2)}) collective-permute-start(bf16[4,64,384]{2,1,0:T(8,128)(2,1)S(1)} %get-tuple-element.38), channel_id=1, source_target_pairs={{0,1},{1,0},{64,65},{65,64},{2,3},{3,2},{66,67},{67,66},{4,5},{5,4... | collective-permute-start | bytes 589832 | tf_op jit(solution)/shard_map/ppermute | solution.py:80
  6.4 19.7 %collective-permute-start.8 = (bf16[16,64,384]{2,1,0:T(8,128)(2,1)S(1)}, bf16[16,64,384]{2,1,0:T(8,128)(2,1)S(1)}, u32[]{:S(2)}, u32[]{:S(2)}) collective-permute-start(bf16[16,64,384]{2,1,0:T(8,128)(2,1)S(1)} %get-tuple-element.46), channel_id=1, source_target_pairs={{1,2},{3,4},{5,6},{7,8},{9,10},{11,12},{13,14},{2,1},{4,3},{6,5},{... | collective-permute-start | bytes 2359304 | tf_op jit(solution)/shard_map/ppermute | solution.py:492
  7.2 18.4 %collective-permute-start.6 = (bf16[8,64,384]{2,1,0:T(8,128)(2,1)S(1)}, bf16[8,64,384]{2,1,0:T(8,128)(2,1)S(1)}, u32[]{:S(2)}, u32[]{:S(2)}) collective-permute-start(bf16[8,64,384]{2,1,0:T(8,128)(2,1)S(1)} %get-tuple-element.72), channel_id=1, source_target_pairs={{1,2},{3,4},{5,6},{7,8},{9,10},{11,12},{13,14},{2,1},{4,3},{6,5},{... | collective-permute-start | bytes 1179656 | tf_op jit(solution)/shard_map/ppermute | solution.py:492
  17.9 13.0 %collective-permute-start.7 = (bf16[8,64,384]{2,1,0:T(8,128)(2,1)S(1)}, bf16[8,64,384]{2,1,0:T(8,128)(2,1)S(1)}, u32[]{:S(2)}, u32[]{:S(2)}) collective-permute-start(bf16[8,64,384]{2,1,0:T(8,128)(2,1)S(1)} %get-tuple-element.71), channel_id=1, source_target_pairs={{1,2},{3,4},{5,6},{7,8},{9,10},{11,12},{13,14},{2,1},{4,3},{6,5},{... | collective-permute-start | bytes 1179656 | tf_op jit(solution)/shard_map/ppermute | solution.py:492
  21.3 36.5 %collective-permute-start.3 = (bf16[32,64,384]{2,1,0:T(8,128)(2,1)S(1)}, bf16[32,64,384]{2,1,0:T(8,128)(2,1)S(1)}, u32[]{:S(2)}, u32[]{:S(2)}) collective-permute-start(bf16[32,64,384]{2,1,0:T(8,128)(2,1)S(1)} %get-tuple-element.42.own_ref.hidden_ref), channel_id=1, source_target_pairs={{1,1},{2,2},{5,5},{6,6},{9,9},{10,10},{13,13},{14,14},{3,7},{4,0},... | collective-permute-start | bytes 4718600 | tf_op jit(solution)/shard_map/ppermute | solution.py:500
  36.6 23.6 %collective-permute-start.9 = (bf16[4,2,216,384]{3,2,1,0:T(8,128)(2,1)S(1)}, bf16[4,2,216,384]{3,2,1,0:T(8,128)(2,1)S(1)}, u32[]{:S(2)}, u32[]{:S(2)}) collective-permute-start(bf16[4,2,216,384]{3,2,1,0:T(8,128)(2,1)S(1)} %get-tuple-element.48), channel_id=1, source_target_pairs={{0,1},{1,0},{64,65},{65,64},{2,3},{3,2},{66,67},{67,66},{4,5},{5,4... | collective-permute-start | bytes 3981320 | tf_op jit(solution)/shard_map/ppermute | solution.py:80
  57.2 5.6 %collective-permute-start.15 = (bf16[4,2,216,384]{3,2,1,0:T(8,128)(2,1)S(1)}, bf16[4,2,216,384]{3,2,1,0:T(8,128)(2,1)S(1)}, u32[]{:S(2)}, u32[]{:S(2)}) collective-permute-start(bf16[4,2,216,384]{3,2,1,0:T(8,128)(2,1)S(1)} %get-tuple-element.57), channel_id=1, source_target_pairs={{0,1},{1,0},{64,65},{65,64},{2,3},{3,2},{66,67},{67,66},{4,5},{5,4... | collective-permute-start | bytes 3981320 | tf_op jit(solution)/shard_map/ppermute | solution.py:80
  57.3 30.3 %collective-permute-start.2 = (bf16[32,64,384]{2,1,0:T(8,128)(2,1)S(1)}, bf16[32,64,384]{2,1,0:T(8,128)(2,1)S(1)}, u32[]{:S(2)}, u32[]{:S(2)}) collective-permute-start(bf16[32,64,384]{2,1,0:T(8,128)(2,1)S(1)} %get-tuple-element.42.own_ref.hidden_ref), channel_id=1, source_target_pairs={{0,1},{1,0},{64,65},{65,64},{2,3},{3,2},{66,67},{67,66},{4,5},{5,4... | collective-permute-start | bytes 4718600 | tf_op jit(solution)/shard_map/ppermute | solution.py:80
  57.8 44.0 %collective-permute-start.4 = (bf16[32,64,384]{2,1,0:T(8,128)(2,1)S(1)}, bf16[32,64,384]{2,1,0:T(8,128)(2,1)S(1)}, u32[]{:S(2)}, u32[]{:S(2)}) collective-permute-start(bf16[32,64,384]{2,1,0:T(8,128)(2,1)S(1)} %collective-permute-done.3), channel_id=1, source_target_pairs={{0,3},{1,2},{2,1},{3,0},{4,7},{5,6},{6,5},{7,4},{8,11},{9,10},{10,... | collective-permute-start | bytes 4718600 | tf_op jit(solution)/shard_map/ppermute | solution.py:501
  61.2 10.8 %collective-permute-start.10 = (bf16[2,2,216,384]{3,2,1,0:T(8,128)(2,1)S(1)}, bf16[2,2,216,384]{3,2,1,0:T(8,128)(2,1)S(1)}, u32[]{:S(2)}, u32[]{:S(2)}) collective-permute-start(bf16[2,2,216,384]{3,2,1,0:T(8,128)(2,1)S(1)} %get-tuple-element.50), channel_id=1, source_target_pairs={{0,16},{1,49},{64,80},{65,113},{2,18},{3,51},{66,82},{67,115},{4,2... | collective-permute-start | bytes 1990664 | tf_op jit(solution)/shard_map/ppermute | solution.py:80
  63.1 11.8 %collective-permute-start.16 = (bf16[2,2,216,384]{3,2,1,0:T(8,128)(2,1)S(1)}, bf16[2,2,216,384]{3,2,1,0:T(8,128)(2,1)S(1)}, u32[]{:S(2)}, u32[]{:S(2)}) collective-permute-start(bf16[2,2,216,384]{3,2,1,0:T(8,128)(2,1)S(1)} %get-tuple-element.59), channel_id=1, source_target_pairs={{0,4},{1,13},{64,68},{65,77},{2,6},{3,15},{66,70},{67,79},{4,0},{5... | collective-permute-start | bytes 1990664 | tf_op jit(solution)/shard_map/ppermute | solution.py:80
  72.1 8.4 %collective-permute-start.11 = (bf16[2,216,384]{2,1,0:T(8,128)(2,1)S(1)}, bf16[2,216,384]{2,1,0:T(8,128)(2,1)S(1)}, u32[]{:S(2)}, u32[]{:S(2)}) collective-permute-start(bf16[2,216,384]{2,1,0:T(8,128)(2,1)S(1)} %shard_map.81), channel_id=1, source_target_pairs={{0,48},{1,17},{64,112},{65,81},{2,50},{3,19},{66,114},{67,83},{4,5... | collective-permute-start | bytes 995336 | tf_op jit(solution)/shard_map/ppermute | solution.py:80
  75.0 9.4 %collective-permute-start.17 = (bf16[2,216,384]{2,1,0:T(8,128)(2,1)S(1)}, bf16[2,216,384]{2,1,0:T(8,128)(2,1)S(1)}, u32[]{:S(2)}, u32[]{:S(2)}) collective-permute-start(bf16[2,216,384]{2,1,0:T(8,128)(2,1)S(1)} %shard_map.88), channel_id=1, source_target_pairs={{0,12},{1,5},{64,76},{65,69},{2,14},{3,7},{66,78},{67,71},{4,8},{5... | collective-permute-start | bytes 995336 | tf_op jit(solution)/shard_map/ppermute | solution.py:80
  81.1 6.9 %collective-permute-start.12 = (bf16[112,384]{1,0:T(8,128)(2,1)S(1)}, bf16[112,384]{1,0:T(8,128)(2,1)S(1)}, u32[]{:S(2)}, u32[]{:S(2)}) collective-permute-start(bf16[112,384]{1,0:T(8,128)(2,1)S(1)} %get-tuple-element.53), channel_id=1, source_target_pairs={{0,4},{1,5},{64,68},{65,69},{2,6},{3,7},{66,70},{67,71},{4,8},{5,9... | collective-permute-start | bytes 258056 | tf_op jit(solution)/shard_map/ppermute | solution.py:80
  82.7 9.2 %collective-permute-start.13 = (bf16[112,384]{1,0:T(8,128)(2,1)S(1)}, bf16[112,384]{1,0:T(8,128)(2,1)S(1)}, u32[]{:S(2)}, u32[]{:S(2)}) collective-permute-start(bf16[112,384]{1,0:T(8,128)(2,1)S(1)} %get-tuple-element.54), channel_id=1, source_target_pairs={{0,8},{1,9},{64,72},{65,73},{2,10},{3,11},{66,74},{67,75},{4,12},{... | collective-permute-start | bytes 258056 | tf_op jit(solution)/shard_map/ppermute | solution.py:80
  84.4 10.5 %collective-permute-start.14 = (bf16[112,384]{1,0:T(8,128)(2,1)S(1)}, bf16[112,384]{1,0:T(8,128)(2,1)S(1)}, u32[]{:S(2)}, u32[]{:S(2)}) collective-permute-start(bf16[112,384]{1,0:T(8,128)(2,1)S(1)} %get-tuple-element.55), channel_id=1, source_target_pairs={{0,12},{1,13},{64,76},{65,77},{2,14},{3,15},{66,78},{67,79},{4,0},... | collective-permute-start | bytes 258056 | tf_op jit(solution)/shard_map/ppermute | solution.py:80
  87.6 7.3 %collective-permute-start.18 = (bf16[112,384]{1,0:T(8,128)(2,1)S(1)}, bf16[112,384]{1,0:T(8,128)(2,1)S(1)}, u32[]{:S(2)}, u32[]{:S(2)}) collective-permute-start(bf16[112,384]{1,0:T(8,128)(2,1)S(1)} %get-tuple-element.62), channel_id=1, source_target_pairs={{0,16},{1,17},{64,80},{65,81},{2,18},{3,19},{66,82},{67,83},{4,20}... | collective-permute-start | bytes 258056 | tf_op jit(solution)/shard_map/ppermute | solution.py:80
  87.9 7.3 %collective-permute-start.19 = (bf16[112,384]{1,0:T(8,128)(2,1)S(1)}, bf16[112,384]{1,0:T(8,128)(2,1)S(1)}, u32[]{:S(2)}, u32[]{:S(2)}) collective-permute-start(bf16[112,384]{1,0:T(8,128)(2,1)S(1)} %get-tuple-element.63), channel_id=1, source_target_pairs={{0,32},{1,33},{64,96},{65,97},{2,34},{3,35},{66,98},{67,99},{4,36}... | collective-permute-start | bytes 258056 | tf_op jit(solution)/shard_map/ppermute | solution.py:80
  91.9 4.5 %collective-permute-start.20 = (bf16[112,384]{1,0:T(8,128)(2,1)S(1)}, bf16[112,384]{1,0:T(8,128)(2,1)S(1)}, u32[]{:S(2)}, u32[]{:S(2)}) collective-permute-start(bf16[112,384]{1,0:T(8,128)(2,1)S(1)} %get-tuple-element.64), channel_id=1, source_target_pairs={{0,48},{1,49},{64,112},{65,113},{2,50},{3,51},{66,114},{67,115},{4... | collective-permute-start | bytes 258056 | tf_op jit(solution)/shard_map/ppermute | solution.py:80
  97.0 7.5 %collective-permute-start.21 = (bf16[216,96]{1,0:T(8,128)(2,1)S(1)}, bf16[216,96]{1,0:T(8,128)(2,1)S(1)}, u32[]{:S(2)}, u32[]{:S(2)}) collective-permute-start(bf16[216,96]{1,0:T(8,128)(2,1)S(1)} %get-tuple-element.66), channel_id=1, source_target_pairs={{0,2},{1,3},{64,66},{65,67},{2,0},{3,1},{66,64},{67,65},{4,6},{5,7... | collective-permute-start | bytes 124424 | tf_op jit(solution)/shard_map/ppermute | solution.py:80
  97.5 7.0 %collective-permute-start.22 = (bf16[216,96]{1,0:T(8,128)(2,1)S(1)}, bf16[216,96]{1,0:T(8,128)(2,1)S(1)}, u32[]{:S(2)}, u32[]{:S(2)}) collective-permute-start(bf16[216,96]{1,0:T(8,128)(2,1)S(1)} %get-tuple-element.67), channel_id=1, source_target_pairs={{0,64},{1,65},{64,0},{65,1},{2,66},{3,67},{66,2},{67,3},{4,68},{5,... | collective-permute-start | bytes 124424 | tf_op jit(solution)/shard_map/ppermute | solution.py:80
  101.4 5.4 %collective-permute-start.23 = (bf16[216,96]{1,0:T(8,128)(2,1)S(1)}, bf16[216,96]{1,0:T(8,128)(2,1)S(1)}, u32[]{:S(2)}, u32[]{:S(2)}) collective-permute-start(bf16[216,96]{1,0:T(8,128)(2,1)S(1)} %get-tuple-element.68), channel_id=1, source_target_pairs={{0,66},{1,67},{64,2},{65,3},{2,64},{3,65},{66,0},{67,1},{4,70},{5,... | collective-permute-start | bytes 124424 | tf_op jit(solution)/shard_map/ppermute | solution.py:80
  (3 other events, 23.7 us)
